TPU v7x, 32 devices: a whole 2x2x4 slice. The times are simulated.
32 devices in a mesh: gx: 4 (over y, x), gy: 4 (over z), gz: 2 (over core).
Axes of the slice: x: 2, y: 2, z: 4, core: 2. Of those that a mesh axis runs over, the one named last changes fastest.
Arguments:
- rhs: float32 [7, 7, 7, 4, 16, 256], P(None, None, None, 'gx', 'gy', 'gz'), may hold values from -6 to 6
- orders: int32 [4, 16, 256], P('gx', 'gy', 'gz'), may hold values from 3 to 6
Outputs:
- smoothed: float32 [7, 7, 7, 4, 16, 256], P(None, None, None, 'gx', 'gy', 'gz')
- coarse_residual: float32 [4, 16, 256], P('gx', 'gy')
All inputs are finite; a program needn't handle non-finite values.
Results may differ from a plain program's by a relative error of at most 0.00016.
Values sent between devices are 32-bit elements; how exact they have to be, the bound alone decides.
A program may use at most 64 MiB of HBM per device.

v0:
```python
import functools

import jax
import jax.numpy as jnp
import numpy as np
from jax import lax
from jax.experimental import pallas as pl
from jax.experimental.pallas import tpu as pltpu
from jax.sharding import PartitionSpec as P

PENALTY = 49.0
EIGEN_HIGH = 2.4
EIGEN_LOW = 0.24
MODES = 7
RELAYED = 3
MESH = pl.DeviceIdType.MESH


def tables():
    degree = np.arange(MODES)
    normed = np.sqrt((2.0 * degree + 1.0) / 2.0)
    smaller = np.minimum(degree[:, None], degree[None, :])
    parity = (degree[:, None] + degree[None, :]) % 2 == 0
    stiffness = np.where(parity, normed[:, None] * normed[None, :] * smaller * (smaller + 1), 0.0)
    signs = (-1.0) ** degree
    slope = normed * degree * (degree + 1) / 2.0
    low, low_slope = normed * signs, -slope * signs
    own = stiffness + np.outer(normed, PENALTY * normed - 0.5 * slope) - 0.5 * np.outer(slope, normed)
    own = own + np.outer(low, PENALTY * low + 0.5 * low_slope) + 0.5 * np.outer(low_slope, low)
    one_axis = normed * normed * degree * (degree + 1) + 2.0 * (
        PENALTY * normed * normed - normed * slope
    )
    diagonal = (
        one_axis[:, None, None] + one_axis[None, :, None] + one_axis[None, None, :]
    ) / PENALTY
    return (
        own / PENALTY,
        0.5 * slope - PENALTY * normed,
        0.5 * normed,
        normed / PENALTY,
        slope / PENALTY,
        diagonal,
    )


OWN, JUMP, HALF, VALUE, SLOPE, DIAGONAL = tables()
THETA = 0.5 * (EIGEN_HIGH + EIGEN_LOW)
DELTA = 0.5 * (EIGEN_HIGH - EIGEN_LOW)
RHO_FIRST = DELTA / THETA
RHO_SECOND = 1.0 / (2.0 * THETA / DELTA - RHO_FIRST)
KEEP = 1.0 + RHO_SECOND * RHO_FIRST
STEP = 2.0 * RHO_SECOND / DELTA * THETA


def combine(weights, values):
    total = None
    for weight, value in zip(weights, values):
        term = value * float(weight)
        total = term if total is None else total + term
    return total


def traces(values):
    even, odd = values[0::2], values[1::2]
    jump_even, jump_odd = combine(JUMP[0::2], even), combine(JUMP[1::2], odd)
    half_even, half_odd = combine(HALF[0::2], even), combine(HALF[1::2], odd)
    down = (jump_even - jump_odd, half_even - half_odd)
    up = (jump_even + jump_odd, half_even + half_odd)
    return down, up


def own_row(row, values):
    start = row % 2
    return combine(OWN[row, start::2], values[start::2])


def face_terms(from_up, from_down):
    both = (from_up[0] + from_down[0], from_up[1] + from_down[1])
    apart = (from_up[0] - from_down[0], from_up[1] - from_down[1])

    def term(mode):
        pair = both if mode % 2 == 0 else apart
        if mode == 0:
            return pair[0] * float(VALUE[0])
        return pair[0] * float(VALUE[mode]) + pair[1] * float(SLOPE[mode])

    return term


def vertex_pair(zero, one):
    flat, tilt = np.sqrt(0.5) * zero, (np.sqrt(1.5) / 3.0) * one
    return flat - tilt, flat + tilt


def kernel(
    sizes, cells_y, cells_z, rhs_hbm, orders_hbm, table_hbm, smooth, coarse_ref,
    rhs, first, acc, orders_ref, table_ref,
    xs, xr, ys, yr, zs, zr, y_up, y_down,
    xs2, xr2, ys2, yr2, zs2, zr2, y_up2, y_down2, acc2, shift_buf,
    main, top, main_in, top_in,
    relay, local_sem, send_sem, recv_sem, x_send, x_recv, relay_in, relay_out,
):
    nx, ny, nz = sizes
    x, y, z = lax.axis_index("gx"), lax.axis_index("gy"), lax.axis_index("gz")
    barrier = pltpu.get_barrier_semaphore()

    def neighbour(axis, sign):
        here = (x, y, z)[axis]
        to = [x, y, z]
        to[axis] = here + sign
        back = [x, y, z]
        back[axis] = here - sign
        below, above = here > 0, here < sizes[axis] - 1
        return (tuple(to), below if sign < 0 else above, tuple(back), above if sign < 0 else below)

    halos = [neighbour(axis, sign) for axis in range(3) for sign in (-1, 1)]
    always = x >= 0
    carries = []
    for i in range(2):
        for j in range(2):
            for r in range(nz):
                if i == 0 and j == 0 and r == 0:
                    continue
                to = (x + i, y + j, lax.rem(z + r, nz))
                source = lax.rem(z - r + nz, nz)
                back = (x - i, y - j, source)
                ok_to, ok_from = always, always
                if i:
                    ok_to, ok_from = ok_to & (x < nx - 1), ok_from & (x > 0)
                if j:
                    ok_to, ok_from = ok_to & (y < ny - 1), ok_from & (y > 0)
                carries.append((to, ok_to, back, ok_from, i, j, source))

    odd = lax.rem(x, 2) == 1
    even = jnp.logical_not(odd)
    relays = (
        ((x - 2, y, z), even & (x >= 2), (x + 2, y, z), even & (x + 2 < nx), (x + 1, y, z)),
        ((x + 2, y, z), odd & (x + 2 < nx), (x - 2, y, z), odd & (x >= 3), (x - 1, y, z)),
    )

    expected = jnp.int32(0)
    for entry in halos + list(relays):
        to, ok_to, back, ok_from = entry[:4]

        @pl.when(ok_from)
        def _(back=back):
            pl.semaphore_signal(barrier, inc=1, device_id=back, device_id_type=MESH)

        expected = expected + jnp.where(ok_to, 1, 0).astype(jnp.int32)

    loads = [
        pltpu.make_async_copy(orders_hbm, orders_ref, local_sem.at[MODES]),
        pltpu.make_async_copy(table_hbm, table_ref, local_sem.at[MODES + 1]),
    ]
    for copy in loads:
        copy.start()

    def rhs_load(b):
        return pltpu.make_async_copy(rhs_hbm.at[:, b], rhs.at[:, b], local_sem.at[b])

    for b in range(MODES):
        rhs_load(b).start()

    def remote(src, dst, slot, to):
        return pltpu.make_async_remote_copy(
            src_ref=src, dst_ref=dst, send_sem=send_sem.at[slot], recv_sem=recv_sem.at[slot],
            device_id=to, device_id_type=MESH,
        )

    def start(index, slot, src, dst):
        to, ok_to = halos[index][:2]

        @pl.when(ok_to)
        def _():
            remote(src, dst, slot, to).start()

    def receive(index, slot, src, dst):
        to, _, _, ok_from = halos[index]

        @pl.when(ok_from)
        def _():
            remote(src, dst, slot, to).wait_recv()

    def finish(index, slot, src, dst):
        to, ok_to = halos[index][:2]

        @pl.when(ok_to)
        def _():
            remote(src, dst, slot, to).wait_send()

    stages = (((xs, xr), (ys, yr), (zs, zr)), ((xs2, xr2), (ys2, yr2), (zs2, zr2)))

    def over(action, stage, axis):
        src, dst = stages[stage][axis]
        for side in range(2):
            index = 2 * axis + side
            action(index, 6 * stage + index, src.at[side], dst.at[side])

    for stage in range(2):
        for axis in range(3):
            for side in range(2):
                dst = stages[stage][axis][1]

                @pl.when(jnp.logical_not(halos[2 * axis + side][3]))
                def _(dst=dst, side=side):
                    dst[side] = jnp.zeros(dst.shape[1:], jnp.float32)

    for copy in loads:
        copy.wait()
    orders = orders_ref[0]
    tile = (MODES, cells_y, cells_z)
    last_mode = lax.broadcasted_iota(jnp.int32, tile, 0)
    lane = lax.broadcasted_iota(jnp.int32, (1, 1, cells_z), 2)

    def active(a, b):
        return jnp.maximum(jnp.maximum(a, b), last_mode) <= orders[None]

    def loop(body):
        def step(index, carry):
            body(index)
            return carry

        lax.fori_loop(0, MODES, step, 0)

    def x_copy(side, b, to):
        return pltpu.make_async_remote_copy(
            src_ref=xs.at[side, b], dst_ref=xr.at[side, b],
            send_sem=x_send.at[side, b], recv_sem=x_recv.at[side, b],
            device_id=to, device_id_type=MESH,
        )

    def to_relay(side, b, to):
        return pltpu.make_async_remote_copy(
            src_ref=xs.at[side, b], dst_ref=relay.at[side, b],
            send_sem=x_send.at[side, b], recv_sem=relay_in.at[side, b],
            device_id=to, device_id_type=MESH,
        )

    def from_relay(side, b, to):
        return pltpu.make_async_remote_copy(
            src_ref=relay.at[side, b], dst_ref=xr.at[side, b],
            send_sem=relay_out.at[side, b], recv_sem=x_recv.at[side, b],
            device_id=to, device_id_type=MESH,
        )

    def x_start(b):
        for side in range(2):
            to, ok_to = halos[side][:2]
            via, used = relays[side][:2]
            detour = used & (b < RELAYED)

            @pl.when(detour)
            def _():
                to_relay(side, b, via).start()

            @pl.when(ok_to & jnp.logical_not(detour))
            def _():
                x_copy(side, b, to).start()

    def forward(b):
        for side in range(2):
            back, relaying, target = relays[side][2:]

            @pl.when(relaying)
            def _():
                to_relay(side, b, target).wait_recv()
                from_relay(side, b, target).start()

    def x_receive(b):
        for side in range(2):

            @pl.when(halos[side][3])
            def _():
                x_copy(side, b, halos[side][0]).wait_recv()

    def x_finish(b):
        for side in range(2):

            @pl.when(halos[side][1])
            def _():
                x_copy(side, b, halos[side][0]).wait_send()

    def relay_finish(b):
        for side in range(2):

            @pl.when(relays[side][3])
            def _():
                from_relay(side, b, relays[side][4]).wait_send()

    pl.semaphore_wait(barrier, expected)

    def x_traces(b):
        rhs_load(b).wait()
        values = []
        for a in range(MODES):
            value = jnp.where(active(a, b), table_ref[a, b] * rhs[a, b], 0.0)
            first[a, b] = value
            values.append(value)
        sides = traces(values)
        for side in range(2):
            for kind in range(2):
                xs[side, b, kind] = sides[side][kind]
        x_start(b)

    loop(x_traces)

    def y_faces(a, values, send, up_buf, down_buf):
        down, up = traces(values)
        for kind in range(2):
            up_buf[kind, a, :, 0:cells_y, :] = down[kind]
            down_buf[kind, a, :, 1 : cells_y + 1, :] = up[kind]
            send[0, kind, a] = down[kind][:, 0:1, :]
            send[1, kind, a] = up[kind][:, cells_y - 1 : cells_y, :]

    def y_neighbours(a, received, up_buf, down_buf):
        for kind in range(2):
            up_buf[kind, a, :, cells_y : cells_y + 1, :] = received[0, kind, a]
            down_buf[kind, a, :, 0:1, :] = received[1, kind, a]
        return face_terms(
            [up_buf[kind, a, :, 1 : cells_y + 1, :] for kind in range(2)],
            [down_buf[kind, a, :, 0:cells_y, :] for kind in range(2)],
        )

    def z_faces(a, values, send):
        sides = traces(values)
        for side in range(2):
            for kind in range(2):
                send[side, kind, a] = sides[side][kind]

    def z_neighbours(a, send, received):
        def moved(side, kind, edge, amount):
            picked = jnp.where(lane == edge, received[side, kind, a], send[side, kind, a])
            return pltpu.roll(picked, amount, 2)

        return face_terms(
            [moved(0, kind, 0, cells_z - 1) for kind in range(2)],
            [moved(1, kind, cells_z - 1, 1) for kind in range(2)],
        )

    loop(lambda a: z_faces(a, [first[a, :, e] for e in range(MODES)], zs))
    over(start, 0, 2)
    loop(lambda a: y_faces(a, [first[a, b] for b in range(MODES)], ys, y_up, y_down))
    over(start, 0, 1)

    def x_own(b):
        values = [first[a, b] for a in range(MODES)]
        for a in range(MODES):
            acc[a, b] = own_row(a, values)

    def y_own(a):
        values = [first[a, b] for b in range(MODES)]
        for b in range(MODES):
            acc[a, b] += own_row(b, values)

    def z_own(a):
        values = [first[a, :, e] for e in range(MODES)]
        for e in range(MODES):
            acc[a, :, e] += own_row(e, values)

    loop(x_own)
    forward(0)
    loop(y_own)
    forward(1)
    loop(z_own)
    forward(2)

    over(receive, 0, 2)

    def z_flux(a):
        term = z_neighbours(a, zs, zr)
        for e in range(MODES):
            acc[a, :, e] += term(e)

    loop(z_flux)
    over(receive, 0, 1)

    def y_flux(a):
        term = y_neighbours(a, yr, y_up, y_down)
        for b in range(MODES):
            acc[a, b] += term(b)

    loop(y_flux)

    def x_flux(index):
        b = lax.rem(index + RELAYED, MODES)
        x_receive(b)
        term = face_terms(
            [xr[0, b, kind] for kind in range(2)], [xr[1, b, kind] for kind in range(2)]
        )
        for a in range(MODES):
            right = rhs[a, b]
            total = acc[a, b] + term(a)
            value = table_ref[a, b] * (KEEP * right + STEP * (right - total))
            smooth[a, b] = jnp.where(active(a, b), value, 0.0)

    loop(x_flux)

    for b in range(2):
        values = [smooth[a, b, 0:2] for a in range(MODES)]
        sides = traces(values)
        for side in range(2):
            for kind in range(2):
                xs2[side, kind, b] = sides[side][kind]
    over(start, 1, 0)
    for a in range(2):
        y_faces(a, [smooth[a, b, 0:2] for b in range(MODES)], ys2, y_up2, y_down2)
    over(start, 1, 1)
    for a in range(2):
        z_faces(a, [smooth[a, 0:2, e] for e in range(MODES)], zs2)
    over(start, 1, 2)
    for b in range(2):
        values = [smooth[a, b, 0:2] for a in range(MODES)]
        for a in range(2):
            acc2[a, b] = own_row(a, values)
    for a in range(2):
        values = [smooth[a, b, 0:2] for b in range(MODES)]
        for b in range(2):
            acc2[a, b] += own_row(b, values)
        values = [smooth[a, 0:2, e] for e in range(MODES)]
        for e in range(2):
            acc2[a, :, e] += own_row(e, values)
    over(receive, 1, 2)
    for a in range(2):
        term = z_neighbours(a, zs2, zr2)
        for e in range(2):
            acc2[a, :, e] += term(e)
    over(receive, 1, 1)
    for a in range(2):
        term = y_neighbours(a, yr2, y_up2, y_down2)
        for b in range(2):
            acc2[a, b] += term(b)
    over(receive, 1, 0)
    for b in range(2):
        term = face_terms(
            [xr2[0, kind, b] for kind in range(2)], [xr2[1, kind, b] for kind in range(2)]
        )
        for a in range(2):
            acc2[a, b] += term(a)

    resid = {}
    for a in range(2):
        for b in range(2):
            for e in range(2):
                left = rhs[a, b, e] - acc2[a, b, e]
                resid[a, b, e] = jnp.where(orders >= max(a, b, e), left, 0.0)
    for axis in range(3):
        done = {}
        for key in resid:
            if key[axis] == 0:
                other = tuple(1 if n == axis else key[n] for n in range(3))
                done[key], done[other] = vertex_pair(resid[key], resid[other])
        resid = done

    for i in range(2):
        for k in range(2):
            shift_buf[i, k, 0:1, :] = jnp.zeros((1, cells_z), jnp.float32)
            shift_buf[i, k, 1 : cells_y + 1, :] = resid[i, 1, k]
            main[i, k] = resid[i, 0, k] + shift_buf[i, k, 0:cells_y, :]
            top[i, k] = resid[i, 1, k][cells_y - 1 : cells_y, :]

    @pl.when(x == 0)
    def _():
        main_in[1] = jnp.zeros(main_in.shape[1:], jnp.float32)
        top_in[1] = jnp.zeros(top_in.shape[1:], jnp.float32)

    @pl.when(y == 0)
    def _():
        top_in[...] = jnp.zeros(top_in.shape, jnp.float32)

    def carry(number, arriving):
        to, _, _, _, i, j, source = carries[number]
        src, dst = (top, top_in) if j else (main, main_in)
        return remote(src.at[i], dst.at[i, source if arriving else z], 12 + number, to)

    for number in range(len(carries)):
        ok_to = carries[number][1]

        @pl.when(ok_to)
        def _(number=number):
            carry(number, False).start()

    main_in[0, pl.ds(z, 1)] = main[0][None]

    for number in range(len(carries)):
        ok_from = carries[number][3]

        @pl.when(ok_from)
        def _(number=number):
            carry(number, True).wait_recv()

    row = lax.broadcasted_iota(jnp.int32, (cells_y, cells_z), 0)
    column = lax.broadcasted_iota(jnp.int32, (cells_y, cells_z), 1)
    below = jnp.zeros((cells_y, cells_z), jnp.float32)
    for zz in range(nz):
        sums = []
        for k in range(2):
            total = main_in[0, zz, k] + main_in[1, zz, k]
            extra = top_in[0, zz, k] + top_in[1, zz, k]
            sums.append(total + jnp.where(row == 0, extra, 0.0))
        moved = pltpu.roll(jnp.where(column == cells_z - 1, below, sums[1]), 1, 1)
        below = sums[1]
        inside = (x > 0) & ((row > 0) | (y > 0))
        if zz == 0:
            inside = inside & (column > 0)
        coarse_ref[0, :, zz * cells_z : (zz + 1) * cells_z] = jnp.where(
            inside, sums[0] + moved, 0.0
        )

    for stage in range(2):
        for axis in range(3):
            if (stage, axis) != (0, 0):
                over(finish, stage, axis)
    loop(x_finish)
    for b in range(RELAYED):
        relay_finish(b)
    for number in range(len(carries)):
        ok_to = carries[number][1]

        @pl.when(ok_to)
        def _(number=number):
            carry(number, False).wait_send()


def per_device(sizes, rhs, orders):
    _, cells_y, cells_z = orders.shape
    nz = sizes[2]
    table = jnp.asarray(
        np.broadcast_to(
            (1.0 / (DIAGONAL * THETA))[:, :, :, None, None], DIAGONAL.shape + (1, cells_z)
        ),
        jnp.float32,
    )
    field = rhs.reshape(rhs.shape[:3] + rhs.shape[4:])
    cells = (cells_y, cells_z)
    rows = 8 * ((cells_y + 8) // 8)

    def buf(*shape):
        return pltpu.VMEM(shape, jnp.float32)

    def halo(n):
        line = (2, 2, n, n)
        x_line = (2, n, 2, n) if n == MODES else line
        return [
            buf(*x_line, *cells), buf(*x_line, *cells),
            buf(*line, 1, cells_z), buf(*line, 1, cells_z),
            buf(*line, *cells), buf(*line, *cells),
            buf(2, n, n, rows, cells_z), buf(2, n, n, rows, cells_z),
        ]

    slots = 12 + 4 * nz - 1
    vmem = pl.BlockSpec(memory_space=pltpu.VMEM)
    hbm = pl.BlockSpec(memory_space=pltpu.HBM)
    smoothed, coarse = pl.pallas_call(
        functools.partial(kernel, sizes, cells_y, cells_z),
        out_shape=(
            pltpu.VMEM(field.shape, jnp.float32),
            pltpu.VMEM((1, cells_y, nz * cells_z), jnp.float32),
        ),
        in_specs=[hbm, hbm, hbm],
        out_specs=(vmem, vmem),
        scratch_shapes=[buf(*field.shape)] * 3
        + [pltpu.VMEM(orders.shape, jnp.int32), buf(*table.shape)]
        + halo(MODES)
        + halo(2)
        + [
            buf(2, 2, 2, *cells), buf(2, 2, rows, cells_z),
            buf(2, 2, *cells), buf(2, 2, 1, cells_z),
            buf(2, nz, 2, *cells), buf(2, nz, 2, 1, cells_z),
            buf(2, RELAYED, 2, MODES, *cells),
            pltpu.SemaphoreType.DMA((MODES + 2,)),
            pltpu.SemaphoreType.DMA((slots,)),
            pltpu.SemaphoreType.DMA((slots,)),
            pltpu.SemaphoreType.DMA((2, MODES)),
            pltpu.SemaphoreType.DMA((2, MODES)),
            pltpu.SemaphoreType.DMA((2, RELAYED)),
            pltpu.SemaphoreType.DMA((2, RELAYED)),
        ],
        compiler_params=pltpu.CompilerParams(collective_id=0, has_side_effects=True),
        name="smoother",
    )(field, orders, table)
    return smoothed.reshape(rhs.shape), coarse


def solution(mesh):
    sizes = tuple(mesh.shape[axis] for axis in ("gx", "gy", "gz"))
    return jax.shard_map(
        functools.partial(per_device, sizes),
        mesh=mesh,
        in_specs=(P(None, None, None, "gx", "gy", "gz"), P("gx", "gy", "gz")),
        out_specs=(P(None, None, None, "gx", "gy", "gz"), P("gx", "gy", None)),
        check_vma=False,
    )
```

profile of v0, /device:TPU:13, one launch (start us, length us, event | category | flops | bytes accessed | tf_op | source)
XLA Modules:
  0.0 20.4 jit_solution(7190475306048822222)
XLA Ops:
  0.6 18.3 %smoother.1 = (f32[7,7,7,4,128]{4,3,2,1,0:T(4,128)S(1)}, f32[1,4,256]{2,1,0:T(4,128)S(1)}) custom-call(f32[7,7,7,4,128]{4,3,2,1,0:T(4,128)} %bitcast.5, s32[1,4,128]{2,1,0:T(4,128)} %orders_hbm.1, f32[7,7,7,1,128]{4,3,2,1,0:T(1,128)} %constant.2.clone.table_hbm), custom_call_target="tpu_custom_call" | custom-call | tf_op jit(solution)/shard_map/smoother/pallas_call | solution.py:553
  18.9 0.9 %copy.8 = f32[7,7,7,1,4,128]{5,4,3,2,1,0:T(4,128)} copy(f32[7,7,7,1,4,128]{5,4,3,2,1,0:T(4,128)S(1)} %bitcast.4) | data formatting | bytes 1404928
  19.8 0.6 %copy.9 = f32[1,4,256]{2,1,0:T(4,128)} copy(f32[1,4,256]{2,1,0:T(4,128)S(1)} %get-tuple-element.9) | data formatting | bytes 8192
where the time goes:
time: 20.5 us; the launch traced here: 20.4 us
  Pallas kernels  18.3 us (89%)
  local copies, waits for them, and re-layouts  1.45 us (7%)
  between operations  0.64 us (3%)
    pallas_call x1, Pallas kernels, per_device(): pl.pallas_call(functools.partial(kernel, sizes, cells_y, cells_z), out_sh...  18.3 us
    unnamed x2, local copies, waits for them, and re-layouts  1.45 us

commit v1 on v0

v1 whole, which is shorter than its diff:
```python
import functools

import jax
import jax.numpy as jnp
import numpy as np
from jax import lax
from jax.experimental import pallas as pl
from jax.experimental.pallas import tpu as pltpu
from jax.sharding import PartitionSpec as P

PENALTY = 49.0
EIGEN_HIGH = 2.4
EIGEN_LOW = 0.24
MODES = 7
MESH = pl.DeviceIdType.MESH


def tables():
    degree = np.arange(MODES)
    normed = np.sqrt((2.0 * degree + 1.0) / 2.0)
    smaller = np.minimum(degree[:, None], degree[None, :])
    parity = (degree[:, None] + degree[None, :]) % 2 == 0
    stiffness = np.where(parity, normed[:, None] * normed[None, :] * smaller * (smaller + 1), 0.0)
    signs = (-1.0) ** degree
    slope = normed * degree * (degree + 1) / 2.0
    low, low_slope = normed * signs, -slope * signs
    own = stiffness + np.outer(normed, PENALTY * normed - 0.5 * slope) - 0.5 * np.outer(slope, normed)
    own = own + np.outer(low, PENALTY * low + 0.5 * low_slope) + 0.5 * np.outer(low_slope, low)
    one_axis = normed * normed * degree * (degree + 1) + 2.0 * (
        PENALTY * normed * normed - normed * slope
    )
    diagonal = (
        one_axis[:, None, None] + one_axis[None, :, None] + one_axis[None, None, :]
    ) / PENALTY
    return (
        own / PENALTY,
        0.5 * slope - PENALTY * normed,
        0.5 * normed,
        normed / PENALTY,
        slope / PENALTY,
        diagonal,
    )


OWN, JUMP, HALF, VALUE, SLOPE, DIAGONAL = tables()
THETA = 0.5 * (EIGEN_HIGH + EIGEN_LOW)
DELTA = 0.5 * (EIGEN_HIGH - EIGEN_LOW)
RHO_FIRST = DELTA / THETA
RHO_SECOND = 1.0 / (2.0 * THETA / DELTA - RHO_FIRST)
KEEP = 1.0 + RHO_SECOND * RHO_FIRST
STEP = 2.0 * RHO_SECOND / DELTA * THETA


def combine(weights, values):
    total = None
    for weight, value in zip(weights, values):
        term = value * float(weight)
        total = term if total is None else total + term
    return total


def traces(values):
    even, odd = values[0::2], values[1::2]
    jump_even, jump_odd = combine(JUMP[0::2], even), combine(JUMP[1::2], odd)
    half_even, half_odd = combine(HALF[0::2], even), combine(HALF[1::2], odd)
    down = (jump_even - jump_odd, half_even - half_odd)
    up = (jump_even + jump_odd, half_even + half_odd)
    return down, up


def own_row(row, values):
    start = row % 2
    return combine(OWN[row, start::2], values[start::2])


def face_terms(from_up, from_down):
    both = (from_up[0] + from_down[0], from_up[1] + from_down[1])
    apart = (from_up[0] - from_down[0], from_up[1] - from_down[1])

    def term(mode):
        pair = both if mode % 2 == 0 else apart
        if mode == 0:
            return pair[0] * float(VALUE[0])
        return pair[0] * float(VALUE[mode]) + pair[1] * float(SLOPE[mode])

    return term


def vertex_pair(zero, one):
    flat, tilt = np.sqrt(0.5) * zero, (np.sqrt(1.5) / 3.0) * one
    return flat - tilt, flat + tilt


def one_sided(data, mode, from_below):
    if mode == 0:
        return data[0] * float(VALUE[0])
    sign = -1.0 if from_below else 1.0
    return data[0] * (sign * float(VALUE[1])) + data[1] * (sign * float(SLOPE[1]))


def corners(values):
    for axis in range(3):
        done = {}
        for key in values:
            if key[axis] == 0:
                other = tuple(1 if n == axis else key[n] for n in range(3))
                done[key], done[other] = vertex_pair(values[key], values[other])
        values = done
    return values


PAIRS = [(a, b) for a in range(2) for b in range(2)]
OCTET = [(a, b, e) for a in range(2) for b in range(2) for e in range(2)]
FIRST_CHUNKS = ((0, 4, 0, 2), (4, MODES, 0, 2), (0, 2, 2, MODES))
LATE = MODES - 2
CHUNKS = len(FIRST_CHUNKS) + LATE


def kernel(
    sizes, cells_y, cells_z, rhs_hbm, orders_hbm, table_hbm, smooth, coarse_ref,
    rhs, first, acc, coef, orders_ref, table_ref,
    xs, xr, ys, yr, zs, zr, y_up, y_down,
    order_line, order_x, order_y, order_z, order_tile, pads,
    out_mid, out_high, out_low, in_mid, in_high, in_low, column,
    relay, local_sem, send_sem, recv_sem, x_send, x_recv, relay_in, relay_out,
):
    nx, ny, nz = sizes
    rows = pads.shape[1]
    x, y, z = lax.axis_index("gx"), lax.axis_index("gy"), lax.axis_index("gz")
    barrier = pltpu.get_barrier_semaphore()

    def neighbour(axis, sign):
        here = (x, y, z)[axis]
        to = [x, y, z]
        to[axis] = here + sign
        back = [x, y, z]
        back[axis] = here - sign
        below, above = here > 0, here < sizes[axis] - 1
        return (tuple(to), below if sign < 0 else above, tuple(back), above if sign < 0 else below)

    halos = [neighbour(axis, sign) for axis in range(3) for sign in (-1, 1)]
    always = x >= 0

    def offset(dx, dy):
        ok_to, ok_from = always, x > 0
        if dx > 0:
            ok_to, ok_from = ok_to & (x + dx < nx), ok_from & (x >= dx)
        else:
            ok_to, ok_from = ok_to & (x + dx > 0), ok_from & (x - dx < nx)
        if dy > 0:
            ok_to, ok_from = ok_to & (y + dy < ny), ok_from & (y >= dy)
        if dy < 0:
            ok_to, ok_from = ok_to & (y + dy >= 0), ok_from & (y - dy < ny)
        return ((x + dx, y + dy, z), ok_to, (x - dx, y - dy, z), ok_from)

    carries = []
    for dx, dy in ((2, 1), (1, 1), (1, -1), (1, 0), (2, 0), (-1, 1), (-1, 0), (0, 1), (0, -1)):
        carries.append(offset(dx, dy) + (dx, dy))
    columns = []
    for r in range(1, nz):
        source = lax.rem(z - r + nz, nz)
        columns.append(((x, y, lax.rem(z + r, nz)), always, (x, y, source), always, source))

    odd = lax.rem(x, 2) == 1
    even = jnp.logical_not(odd)
    relays = (
        ((x - 2, y, z), even & (x >= 2), (x + 2, y, z), even & (x + 2 < nx), (x + 1, y, z)),
        ((x + 2, y, z), odd & (x + 2 < nx), (x - 2, y, z), odd & (x >= 3), (x - 1, y, z)),
    )

    expected = jnp.int32(0)
    for entry in halos[:4] + columns + list(relays) + carries[:1]:
        to, ok_to, back, ok_from = entry[:4]

        @pl.when(ok_from)
        def _(back=back):
            pl.semaphore_signal(barrier, inc=1, device_id=back, device_id_type=MESH)

        expected = expected + jnp.where(ok_to, 1, 0).astype(jnp.int32)

    loads = [
        pltpu.make_async_copy(orders_hbm, orders_ref, local_sem.at[MODES]),
        pltpu.make_async_copy(table_hbm, table_ref, local_sem.at[MODES + 1]),
    ]
    for copy in loads:
        copy.start()

    def rhs_load(b):
        return pltpu.make_async_copy(rhs_hbm.at[:, b], rhs.at[:, b], local_sem.at[b])

    for b in range(MODES):
        rhs_load(b).start()

    def remote(src, dst, slot, to):
        return pltpu.make_async_remote_copy(
            src_ref=src, dst_ref=dst, send_sem=send_sem.at[slot], recv_sem=recv_sem.at[slot],
            device_id=to, device_id_type=MESH,
        )

    def start(entry, slot, src, dst):
        to, ok_to = entry[:2]

        @pl.when(ok_to)
        def _():
            remote(src, dst, slot, to).start()

    def receive(entry, slot, src, dst):
        to, _, _, ok_from = entry[:4]

        @pl.when(ok_from)
        def _():
            remote(src, dst, slot, to).wait_recv()

    def finish(entry, slot, src, dst):
        to, ok_to = entry[:2]

        @pl.when(ok_to)
        def _():
            remote(src, dst, slot, to).wait_send()

    stages = (
        ((xs, xr), (ys, yr), (zs, zr)),
        ((orders_ref, order_x), (order_line, order_y), (orders_ref, order_z)),
    )

    def over(action, stage, axis):
        src, dst = stages[stage][axis]
        for side in range(2):
            index = 2 * axis + side
            action(halos[index], 6 * stage + index, src.at[0 if src is orders_ref else side], dst.at[side])

    for stage, empty in ((0, 0.0), (1, -1)):
        for axis in range(3):
            for side in range(2):
                dst = stages[stage][axis][1]

                @pl.when(jnp.logical_not(halos[2 * axis + side][3]))
                def _(dst=dst, side=side, empty=empty):
                    dst[side] = jnp.full(dst.shape[1:], empty, dst.dtype)

    pads[...] = jnp.zeros(pads.shape, jnp.float32)
    order_tile[...] = jnp.full(order_tile.shape, -1, jnp.int32)
    targets = {0: (out_mid, in_mid), 1: (out_high, in_high), -1: (out_low, in_low)}

    def carry_refs(dx, dy):
        src, dst = targets[dy]
        at = dx if dy < 0 else dx + 1
        return src.at[at], dst.at[at]

    for _, _, _, ok_from, dx, dy in carries:

        @pl.when(jnp.logical_not(ok_from))
        def _(dx=dx, dy=dy):
            dst = carry_refs(dx, dy)[1]
            dst[...] = jnp.zeros(dst.shape, jnp.float32)

    for copy in loads:
        copy.wait()
    orders = orders_ref[0]
    order_line[0] = orders[0:1]
    order_line[1] = orders[cells_y - 1 : cells_y]
    tile = (MODES, cells_y, cells_z)
    last_mode = lax.broadcasted_iota(jnp.int32, tile, 0)
    lane = lax.broadcasted_iota(jnp.int32, (1, 1, cells_z), 2)

    def active(a, b):
        return jnp.maximum(jnp.maximum(a, b), last_mode) <= orders[None]

    def loop(body, low=0, high=MODES):
        def step(index, carry):
            body(index)
            return carry

        lax.fori_loop(low, high, step, 0)

    def chunk(ref, side, number):
        if isinstance(number, int) and number < len(FIRST_CHUNKS):
            b0, b1, e0, e1 = FIRST_CHUNKS[number]
            return ref.at[side, b0:b1, :, e0:e1]
        return ref.at[side, number - len(FIRST_CHUNKS) + 2, :, 2:MODES]

    def x_copy(side, number, to):
        return pltpu.make_async_remote_copy(
            src_ref=chunk(xs, side, number), dst_ref=chunk(xr, side, number),
            send_sem=x_send.at[side, number], recv_sem=x_recv.at[side, number],
            device_id=to, device_id_type=MESH,
        )

    def to_relay(side, number, to):
        late = number - len(FIRST_CHUNKS)
        return pltpu.make_async_remote_copy(
            src_ref=chunk(xs, side, number), dst_ref=relay.at[side, late],
            send_sem=x_send.at[side, number], recv_sem=relay_in.at[side, late],
            device_id=to, device_id_type=MESH,
        )

    def from_relay(side, number, to):
        late = number - len(FIRST_CHUNKS)
        return pltpu.make_async_remote_copy(
            src_ref=relay.at[side, late], dst_ref=chunk(xr, side, number),
            send_sem=relay_out.at[side, late], recv_sem=x_recv.at[side, number],
            device_id=to, device_id_type=MESH,
        )

    def forward(number):
        for side in range(2):
            back, relaying, target = relays[side][2:]

            @pl.when(relaying)
            def _():
                to_relay(side, number, target).wait_recv()
                from_relay(side, number, target).start()

    def x_receive(number):
        for side in range(2):

            @pl.when(halos[side][3])
            def _():
                x_copy(side, number, halos[side][0]).wait_recv()

    def x_traces(b):
        rhs_load(b).wait()
        values = []
        for a in range(MODES):
            value = jnp.where(active(a, b), table_ref[a, b] * rhs[a, b], 0.0)
            first[a, b] = value
            values.append(value)
        sides = traces(values)
        for side in range(2):
            for kind in range(2):
                xs[side, b, kind] = sides[side][kind]

    loop(x_traces)
    pl.semaphore_wait(barrier, expected)

    def x_start(number, wanted):
        for side in range(2):
            to, ok_to = halos[side][:2]
            via, used = relays[side][:2]
            if wanted == "relayed":

                @pl.when(used)
                def _():
                    to_relay(side, number, via).start()
            elif wanted == "two hops":

                @pl.when(used)
                def _():
                    x_copy(side, number, to).start()
            else:

                @pl.when(ok_to & jnp.logical_not(used))
                def _():
                    x_copy(side, number, to).start()

    early = range(len(FIRST_CHUNKS))
    late = range(len(FIRST_CHUNKS), CHUNKS)
    for number in early:
        x_start(number, "two hops")
        x_start(number, "direct")
    over(start, 1, 0)
    for number in late:
        x_start(number, "relayed")
        x_start(number, "direct")
    over(start, 1, 2)
    over(start, 1, 1)

    def y_faces(a, values, send, up_buf, down_buf):
        down, up = traces(values)
        for kind in range(2):
            up_buf[kind, a, :, 0:cells_y, :] = down[kind]
            down_buf[kind, a, :, 1 : cells_y + 1, :] = up[kind]
            send[0, kind, a] = down[kind][:, 0:1, :]
            send[1, kind, a] = up[kind][:, cells_y - 1 : cells_y, :]

    def y_neighbours(a, received, up_buf, down_buf):
        for kind in range(2):
            up_buf[kind, a, :, cells_y : cells_y + 1, :] = received[0, kind, a]
            down_buf[kind, a, :, 0:1, :] = received[1, kind, a]
        return face_terms(
            [up_buf[kind, a, :, 1 : cells_y + 1, :] for kind in range(2)],
            [down_buf[kind, a, :, 0:cells_y, :] for kind in range(2)],
        )

    def z_faces(a, values, send):
        sides = traces(values)
        for side in range(2):
            for kind in range(2):
                send[side, kind, a] = sides[side][kind]

    def z_neighbours(a, send, received):
        def moved(side, kind, edge, amount):
            picked = jnp.where(lane == edge, received[side, kind, a], send[side, kind, a])
            return pltpu.roll(picked, amount, 2)

        return face_terms(
            [moved(0, kind, 0, cells_z - 1) for kind in range(2)],
            [moved(1, kind, cells_z - 1, 1) for kind in range(2)],
        )

    loop(lambda a: y_faces(a, [first[a, b] for b in range(MODES)], ys, y_up, y_down))
    over(start, 0, 1)
    loop(lambda a: z_faces(a, [first[a, :, e] for e in range(MODES)], zs))
    over(start, 0, 2)

    def x_own(b):
        values = [first[a, b] for a in range(MODES)]
        for a in range(MODES):
            acc[a, b] = own_row(a, values)

    def y_own(a):
        values = [first[a, b] for b in range(MODES)]
        for b in range(MODES):
            acc[a, b] += own_row(b, values)

    def z_own(a):
        values = [first[a, :, e] for e in range(MODES)]
        for e in range(MODES):
            acc[a, :, e] += own_row(e, values)

    loop(x_own)
    loop(y_own)
    loop(z_own)
    over(receive, 0, 2)

    def z_flux(a):
        term = z_neighbours(a, zs, zr)
        for e in range(MODES):
            acc[a, :, e] += term(e)

    loop(z_flux)
    over(receive, 0, 1)

    def y_flux(a):
        term = y_neighbours(a, yr, y_up, y_down)
        for b in range(MODES):
            right = rhs[a, b]
            total = acc[a, b] + term(b)
            scale = jnp.where(active(a, b), table_ref[a, b], 0.0)
            acc[a, b] = scale * (KEEP * right + STEP * (right - total))
            coef[a, b] = scale * (-STEP)

    loop(y_flux)

    for axis in range(3):
        over(receive, 1, axis)
    order_tile[1 : cells_y + 1] = orders
    order_tile[0:1] = order_y[1]
    order_tile[cells_y + 1 : cells_y + 2] = order_y[0]
    for number in late:
        forward(number)
    for number in early:
        x_receive(number)

    def update(a, b, low, high, term):
        part = slice(low, high)
        smooth[a, b, part] = acc[a, b, part] + coef[a, b, part] * term(a)

    def x_terms(b, low, high):
        part = slice(low, high)
        return face_terms(
            [xr[0, b, kind, part] for kind in range(2)], [xr[1, b, kind, part] for kind in range(2)]
        )

    for b in range(2):
        term = x_terms(b, 0, MODES)
        for a in range(2):
            update(a, b, 0, MODES, term)
        term = x_terms(b, 0, 2)
        for a in range(2, MODES):
            update(a, b, 0, 2, term)
    for b in range(2, MODES):
        term = x_terms(b, 0, 2)
        for a in range(2):
            update(a, b, 0, 2, term)

    centre, edge, x_low, x_high, y_low, y_high = {}, {}, {}, {}, {}, {}
    edge_orders = jnp.where(lane[0] == cells_z - 1, order_z[1], order_z[0])
    for key in OCTET:
        centre[key] = rhs[key]
    for b in range(2):
        values = [smooth[a, b, 0:2] for a in range(MODES)]
        down, up = traces(values)
        for a in range(2):
            own = own_row(a, values)
            below, above = one_sided(down, a, False), one_sided(up, a, True)
            for e in range(2):
                centre[a, b, e] = centre[a, b, e] - own[e]
                x_low[a, b, e] = jnp.where(order_x[1] >= max(a, b, e), -below[e], 0.0)
                x_high[a, b, e] = jnp.where(order_x[0] >= max(a, b, e), -above[e], 0.0)
    for a in range(2):
        values = [smooth[a, b, 0:2] for b in range(MODES)]
        down, up = traces(values)
        for b in range(2):
            own = own_row(b, values)
            below, above = one_sided(down, b, False), one_sided(up, b, True)
            for e in range(2):
                centre[a, b, e] = centre[a, b, e] - own[e]
                y_low[a, b, e], y_high[a, b, e] = below[e], above[e]
        values = [smooth[a, 0:2, e] for e in range(MODES)]
        down, up = traces(values)
        for e in range(2):
            below = pltpu.roll(one_sided(down, e, False), cells_z - 1, 2)
            above = pltpu.roll(one_sided(up, e, True), 1, 2)
            inner = jnp.where(lane == cells_z - 1, 0.0, below) + jnp.where(lane == 0, 0.0, above)
            outer = jnp.where(lane == cells_z - 1, below, jnp.where(lane == 0, above, 0.0))
            own = own_row(e, values) + inner
            for b in range(2):
                centre[a, b, e] = centre[a, b, e] - own[b]
                edge[a, b, e] = jnp.where(edge_orders >= max(a, b, e), -outer[b], 0.0)

    slots = iter(range(pads.shape[0]))

    def padded(value, at):
        slot = next(slots)
        pads[slot, at : at + cells_y, :] = value
        return pads[slot]

    own_tile = order_tile[...]
    resid = {}
    for key in OCTET:
        total = padded(centre[key], 1) - padded(y_low[key], 0) - padded(y_high[key], 2)
        resid[key] = jnp.where(own_tile >= max(key), total, 0.0)
    resid = corners(resid)
    near = {key: (corners(x_low)[key], corners(x_high)[key]) for key in OCTET}
    edge = corners(edge)
    row_lane = lane[0]
    sums = {}
    for dx in range(-1, 3):
        layers = []
        for k in range(2):
            parts = []
            if dx in (0, 1):
                parts += [resid[dx, 0, k], pltpu.roll(resid[dx, 1, k], 1, 0)]
            for side, i in ((0, dx + 1), (1, dx - 1)):
                if i in (0, 1):
                    parts += [padded(near[i, j, k][side], 1 + j) for j in range(2)]
            layers.append(functools.reduce(lambda p, q: p + q, parts))
        moved = pltpu.roll(layers[1], 1, 1)
        if dx in (0, 1):
            outer = [padded(edge[dx, 0, k], 1) + padded(edge[dx, 1, k], 2) for k in range(2)]
            outer_moved = pltpu.roll(outer[1], 1, 1)
            inside = layers[0] + jnp.where(row_lane == 0, outer_moved, moved)
            beyond = jnp.where(row_lane == 0, moved, outer_moved) + outer[0]
        else:
            inside = layers[0] + jnp.where(row_lane == 0, 0.0, moved)
            beyond = jnp.where(row_lane == 0, moved, 0.0)
        for part, value in enumerate((inside, beyond)):
            if dx == 0:
                sums[part] = value[1 : cells_y + 1]
            else:
                out_mid[dx + 1, part] = value[1 : cells_y + 1]
            out_high[dx + 1, part] = value[cells_y + 1 : cells_y + 3]
            if dx in (0, 1):
                out_low[dx, part] = value[0:1]

    for number, entry in enumerate(carries):
        start(entry, 12 + number, *carry_refs(*entry[4:]))

    def late_flux(b):
        x_receive(b - 2 + len(FIRST_CHUNKS))
        term = x_terms(b, 2, MODES)
        for a in range(2):
            update(a, b, 2, MODES, term)
        term = x_terms(b, 0, MODES)
        for a in range(2, MODES):
            update(a, b, 0, MODES, term)

    for b in range(2):
        term = x_terms(b, 2, MODES)
        for a in range(2, MODES):
            update(a, b, 2, MODES, term)
    loop(late_flux, 2)

    for number, entry in enumerate(carries):
        receive(entry, 12 + number, *carry_refs(*entry[4:]))

    for part in range(2):
        value = sums[part]
        for at in (0, 2, 3):
            value = value + in_mid[at, part]
        high = in_high[0, part] + in_high[1, part] + in_high[2, part] + in_high[3, part]
        low = in_low[0, part] + in_low[1, part]
        column[pl.ds(z, 1), part] = value[None]
        column[pl.ds(z, 1), part, 0:2] += high[None]
        column[pl.ds(z, 1), part, cells_y - 1 : cells_y] += low[None]

    def gather(number, arriving):
        entry = columns[number]
        at = entry[4] if arriving else z
        return remote(column.at[at], column.at[at], 12 + len(carries) + number, entry[0])

    for number in range(len(columns)):
        gather(number, False).start()
    for number in range(len(columns)):
        gather(number, True).wait_recv()

    row = lax.broadcasted_iota(jnp.int32, (cells_y, cells_z), 0)
    spot = lax.broadcasted_iota(jnp.int32, (cells_y, cells_z), 1)
    for zz in range(nz):
        total = column[zz, 0]
        if zz > 0:
            total = total + jnp.where(spot < 2, column[zz - 1, 1], 0.0)
        if zz < nz - 1:
            total = total + jnp.where(spot == cells_z - 1, column[zz + 1, 1], 0.0)
        inside = (x > 0) & ((row > 0) | (y > 0))
        if zz == 0:
            inside = inside & (spot > 0)
        coarse_ref[0, :, zz * cells_z : (zz + 1) * cells_z] = jnp.where(inside, total, 0.0)

    for stage in range(2):
        for axis in range(3):
            if (stage, axis) != (0, 0):
                over(finish, stage, axis)
    for number in range(CHUNKS):
        for side in range(2):

            @pl.when(halos[side][1])
            def _():
                x_copy(side, number, halos[side][0]).wait_send()

    for number in late:
        for side in range(2):

            @pl.when(relays[side][3])
            def _():
                from_relay(side, number, relays[side][4]).wait_send()

    for number, entry in enumerate(carries):
        finish(entry, 12 + number, *carry_refs(*entry[4:]))
    for number in range(len(columns)):
        gather(number, False).wait_send()


def drain(smooth, coarse, smooth_hbm, coarse_hbm, sem):
    copies = [
        pltpu.make_async_copy(smooth.at[a], smooth_hbm.at[a], sem.at[a]) for a in range(MODES)
    ]
    copies.append(pltpu.make_async_copy(coarse, coarse_hbm, sem.at[MODES]))
    for copy in copies:
        copy.start()
    for copy in copies:
        copy.wait()


def per_device(sizes, rhs, orders):
    _, cells_y, cells_z = orders.shape
    nz = sizes[2]
    table = jnp.asarray(
        np.broadcast_to(
            (1.0 / (DIAGONAL * THETA))[:, :, :, None, None], DIAGONAL.shape + (1, cells_z)
        ),
        jnp.float32,
    )
    field = rhs.reshape(rhs.shape[:3] + rhs.shape[4:])
    cells = (cells_y, cells_z)
    rows = 8 * ((cells_y + 8) // 8)
    tall = 8 * ((cells_y + 10) // 8)
    line = (2, 2, MODES, MODES)

    def buf(*shape):
        return pltpu.VMEM(shape, jnp.float32)

    def whole(*shape):
        return pltpu.VMEM(shape, jnp.int32)

    slots = 12 + 9 + nz - 1
    coarse_shape = (1, cells_y, nz * cells_z)
    vmem = pl.BlockSpec(memory_space=pltpu.VMEM)
    hbm = pl.BlockSpec(memory_space=pltpu.HBM)
    smoothed, coarse = pl.pallas_call(
        functools.partial(kernel, sizes, cells_y, cells_z),
        out_shape=(pltpu.VMEM(field.shape, jnp.float32), pltpu.VMEM(coarse_shape, jnp.float32)),
        in_specs=[hbm, hbm, hbm],
        out_specs=(vmem, vmem),
        scratch_shapes=[buf(*field.shape)] * 4
        + [
            whole(*orders.shape), buf(*table.shape),
            buf(2, MODES, 2, MODES, *cells), buf(2, MODES, 2, MODES, *cells),
            buf(*line, 1, cells_z), buf(*line, 1, cells_z),
            buf(*line, *cells), buf(*line, *cells),
            buf(2, MODES, MODES, rows, cells_z), buf(2, MODES, MODES, rows, cells_z),
            whole(2, 1, cells_z), whole(2, *cells), whole(2, 1, cells_z), whole(2, *cells),
            whole(tall, cells_z), buf(48, tall, cells_z),
            buf(4, 2, *cells), buf(4, 2, 2, cells_z), buf(2, 2, 1, cells_z),
            buf(4, 2, *cells), buf(4, 2, 2, cells_z), buf(2, 2, 1, cells_z),
            buf(nz, 2, *cells),
            buf(2, LATE, 2, LATE, *cells),
            pltpu.SemaphoreType.DMA((MODES + 2,)),
            pltpu.SemaphoreType.DMA((slots,)),
            pltpu.SemaphoreType.DMA((slots,)),
            pltpu.SemaphoreType.DMA((2, CHUNKS)),
            pltpu.SemaphoreType.DMA((2, CHUNKS)),
            pltpu.SemaphoreType.DMA((2, LATE)),
            pltpu.SemaphoreType.DMA((2, LATE)),
        ],
        compiler_params=pltpu.CompilerParams(collective_id=0, has_side_effects=True),
        name="smoother",
    )(field, orders, table)
    smoothed, coarse = pl.pallas_call(
        drain,
        out_shape=(
            jax.ShapeDtypeStruct(field.shape, jnp.float32),
            jax.ShapeDtypeStruct(coarse_shape, jnp.float32),
        ),
        in_specs=[vmem, vmem],
        out_specs=(hbm, hbm),
        scratch_shapes=[pltpu.SemaphoreType.DMA((MODES + 1,))],
        name="drain",
    )(
        pltpu.with_memory_space_constraint(smoothed, pltpu.VMEM),
        pltpu.with_memory_space_constraint(coarse, pltpu.VMEM),
    )
    return smoothed.reshape(rhs.shape), coarse


def solution(mesh):
    sizes = tuple(mesh.shape[axis] for axis in ("gx", "gy", "gz"))
    return jax.shard_map(
        functools.partial(per_device, sizes),
        mesh=mesh,
        in_specs=(P(None, None, None, "gx", "gy", "gz"), P("gx", "gy", "gz")),
        out_specs=(P(None, None, None, "gx", "gy", "gz"), P("gx", "gy", None)),
        check_vma=False,
    )
```

time: 20.5 us -> 17.5 us (0.85)
  the two profiles are of different devices: /device:TPU:13 before, /device:TPU:3 now
where the time goes in v1:
time: 17.5 us; the launch traced here: 17.3 us
  Pallas kernels  16.7 us (95%)
  between operations  0.64 us (4%)
    pallas_call x1, Pallas kernels, per_device(): pl.pallas_call(functools.partial(kernel, sizes, cells_y, cells_z), out_sh...  15.8 us
    pallas_call x1, Pallas kernels, per_device(): pl.pallas_call(drain, out_shape=(jax.ShapeDtypeStruct(field.shape, jnp.fl...  0.91 us

profile of v1, /device:TPU:3, one launch (start us, length us, event | category | flops | bytes accessed | tf_op | source)
XLA Modules:
  0.0 17.3 jit_solution(7055714750140880799)
XLA Ops:
  0.6 15.8 %smoother.1 = (f32[7,7,7,4,128]{4,3,2,1,0:T(4,128)S(1)}, f32[1,4,256]{2,1,0:T(4,128)S(1)}) custom-call(f32[7,7,7,4,128]{4,3,2,1,0:T(4,128)} %bitcast.4, s32[1,4,128]{2,1,0:T(4,128)} %orders_hbm.1, f32[7,7,7,1,128]{4,3,2,1,0:T(1,128)} %constant.2.clone.table_hbm), custom_call_target="tpu_custom_call" | custom-call | tf_op jit(solution)/shard_map/smoother/pallas_call | solution.py:671
  16.4 0.9 %drain.1 = (f32[7,7,7,4,128]{4,3,2,1,0:T(4,128)}, f32[1,4,256]{2,1,0:T(4,128)}) custom-call(f32[7,7,7,4,128]{4,3,2,1,0:T(4,128)S(1)} %get-tuple-element.6.smooth, f32[1,4,256]{2,1,0:T(4,128)S(1)} %get-tuple-element.7.coarse), custom_call_target="tpu_custom_call" | custom-call | tf_op jit(solution)/shard_map/drain/pallas_call | solution.py:700

commit v2 on v1

--- a/solution.py
+++ b/solution.py
@@ -94,8 +94,8 @@
 def one_sided(data, mode, from_below):
     if mode == 0:
         return data[0] * float(VALUE[0])
-    sign = -1.0 if from_below else 1.0
-    return data[0] * (sign * float(VALUE[1])) + data[1] * (sign * float(SLOPE[1]))
+    sign = -1.0 if from_below and mode % 2 else 1.0
+    return data[0] * (sign * float(VALUE[mode])) + data[1] * (sign * float(SLOPE[mode]))
 
 
 def corners(values):
@@ -109,23 +109,25 @@
     return values
 
 
-PAIRS = [(a, b) for a in range(2) for b in range(2)]
 OCTET = [(a, b, e) for a in range(2) for b in range(2) for e in range(2)]
-FIRST_CHUNKS = ((0, 4, 0, 2), (4, MODES, 0, 2), (0, 2, 2, MODES))
-LATE = MODES - 2
-CHUNKS = len(FIRST_CHUNKS) + LATE
+RELAYED = 4
+REACH = range(-2, 4)
+CARRIES = (
+    (3, 1), (2, 1), (-2, 1), (1, 1), (-1, 1), (2, -1), (1, -1), (-1, -1),
+    (3, 0), (2, 0), (-2, 0), (1, 0), (-1, 0), (0, 1), (0, -1),
+)
 
 
 def kernel(
     sizes, cells_y, cells_z, rhs_hbm, orders_hbm, table_hbm, smooth, coarse_ref,
     rhs, first, acc, coef, orders_ref, table_ref,
     xs, xr, ys, yr, zs, zr, y_up, y_down,
-    order_line, order_x, order_y, order_z, order_tile, pads,
+    order_line, order_x, order_y, order_z, pack, pack_in, pads,
     out_mid, out_high, out_low, in_mid, in_high, in_low, column,
     relay, local_sem, send_sem, recv_sem, x_send, x_recv, relay_in, relay_out,
 ):
     nx, ny, nz = sizes
-    rows = pads.shape[1]
+    tall = pads.shape[1]
     x, y, z = lax.axis_index("gx"), lax.axis_index("gy"), lax.axis_index("gz")
     barrier = pltpu.get_barrier_semaphore()
 
@@ -142,20 +144,15 @@
     always = x >= 0
 
     def offset(dx, dy):
-        ok_to, ok_from = always, x > 0
-        if dx > 0:
-            ok_to, ok_from = ok_to & (x + dx < nx), ok_from & (x >= dx)
-        else:
-            ok_to, ok_from = ok_to & (x + dx > 0), ok_from & (x - dx < nx)
+        ok_to = (x + dx > 0) & (x + dx < nx)
+        ok_from = (x > 0) & (x - dx >= 0) & (x - dx < nx)
         if dy > 0:
             ok_to, ok_from = ok_to & (y + dy < ny), ok_from & (y >= dy)
         if dy < 0:
             ok_to, ok_from = ok_to & (y + dy >= 0), ok_from & (y - dy < ny)
         return ((x + dx, y + dy, z), ok_to, (x - dx, y - dy, z), ok_from)
 
-    carries = []
-    for dx, dy in ((2, 1), (1, 1), (1, -1), (1, 0), (2, 0), (-1, 1), (-1, 0), (0, 1), (0, -1)):
-        carries.append(offset(dx, dy) + (dx, dy))
+    carries = [offset(dx, dy) + (dx, dy) for dx, dy in CARRIES]
     columns = []
     for r in range(1, nz):
         source = lax.rem(z - r + nz, nz)
@@ -221,6 +218,7 @@
     stages = (
         ((xs, xr), (ys, yr), (zs, zr)),
         ((orders_ref, order_x), (order_line, order_y), (orders_ref, order_z)),
+        ((pack, pack_in),),
     )
 
     def over(action, stage, axis):
@@ -229,8 +227,8 @@
             index = 2 * axis + side
             action(halos[index], 6 * stage + index, src.at[0 if src is orders_ref else side], dst.at[side])
 
-    for stage, empty in ((0, 0.0), (1, -1)):
-        for axis in range(3):
+    for stage, empty in ((0, 0.0), (1, -1), (2, -1)):
+        for axis in range(len(stages[stage])):
             for side in range(2):
                 dst = stages[stage][axis][1]
 
@@ -239,12 +237,12 @@
                     dst[side] = jnp.full(dst.shape[1:], empty, dst.dtype)
 
     pads[...] = jnp.zeros(pads.shape, jnp.float32)
-    order_tile[...] = jnp.full(order_tile.shape, -1, jnp.int32)
+    pack[...] = jnp.full(pack.shape, -1, jnp.int32)
     targets = {0: (out_mid, in_mid), 1: (out_high, in_high), -1: (out_low, in_low)}
 
     def carry_refs(dx, dy):
         src, dst = targets[dy]
-        at = dx if dy < 0 else dx + 1
+        at = dx + 1 if dy < 0 else dx + 2
         return src.at[at], dst.at[at]
 
     for _, _, _, ok_from, dx, dy in carries:
@@ -273,32 +271,24 @@
 
         lax.fori_loop(low, high, step, 0)
 
-    def chunk(ref, side, number):
-        if isinstance(number, int) and number < len(FIRST_CHUNKS):
-            b0, b1, e0, e1 = FIRST_CHUNKS[number]
-            return ref.at[side, b0:b1, :, e0:e1]
-        return ref.at[side, number - len(FIRST_CHUNKS) + 2, :, 2:MODES]
-
-    def x_copy(side, number, to):
+    def x_copy(side, b, to):
         return pltpu.make_async_remote_copy(
-            src_ref=chunk(xs, side, number), dst_ref=chunk(xr, side, number),
-            send_sem=x_send.at[side, number], recv_sem=x_recv.at[side, number],
+            src_ref=xs.at[side, b], dst_ref=xr.at[side, b],
+            send_sem=x_send.at[side, b], recv_sem=x_recv.at[side, b],
             device_id=to, device_id_type=MESH,
         )
 
-    def to_relay(side, number, to):
-        late = number - len(FIRST_CHUNKS)
+    def to_relay(side, b, to):
         return pltpu.make_async_remote_copy(
-            src_ref=chunk(xs, side, number), dst_ref=relay.at[side, late],
-            send_sem=x_send.at[side, number], recv_sem=relay_in.at[side, late],
+            src_ref=xs.at[side, b], dst_ref=relay.at[side, b],
+            send_sem=x_send.at[side, b], recv_sem=relay_in.at[side, b],
             device_id=to, device_id_type=MESH,
         )
 
-    def from_relay(side, number, to):
-        late = number - len(FIRST_CHUNKS)
+    def from_relay(side, b, to):
         return pltpu.make_async_remote_copy(
-            src_ref=relay.at[side, late], dst_ref=chunk(xr, side, number),
-            send_sem=relay_out.at[side, late], recv_sem=x_recv.at[side, number],
+            src_ref=relay.at[side, b], dst_ref=xr.at[side, b],
+            send_sem=relay_out.at[side, b], recv_sem=x_recv.at[side, b],
             device_id=to, device_id_type=MESH,
         )
 
@@ -330,40 +320,31 @@
             for kind in range(2):
                 xs[side, b, kind] = sides[side][kind]
 
-    loop(x_traces)
-    pl.semaphore_wait(barrier, expected)
-
-    def x_start(number, wanted):
+    def x_start(b):
         for side in range(2):
             to, ok_to = halos[side][:2]
             via, used = relays[side][:2]
-            if wanted == "relayed":
+            if b < RELAYED:
 
                 @pl.when(used)
                 def _():
-                    to_relay(side, number, via).start()
-            elif wanted == "two hops":
-
-                @pl.when(used)
-                def _():
-                    x_copy(side, number, to).start()
-            else:
-
-                @pl.when(ok_to & jnp.logical_not(used))
-                def _():
-                    x_copy(side, number, to).start()
-
-    early = range(len(FIRST_CHUNKS))
-    late = range(len(FIRST_CHUNKS), CHUNKS)
-    for number in early:
-        x_start(number, "two hops")
-        x_start(number, "direct")
+                    to_relay(side, b, via).start()
+
+                ok_to = ok_to & jnp.logical_not(used)
+
+            @pl.when(ok_to)
+            def _():
+                x_copy(side, b, to).start()
+
+    loop(x_traces, 0, 2)
+    pl.semaphore_wait(barrier, expected)
     over(start, 1, 0)
-    for number in late:
-        x_start(number, "relayed")
-        x_start(number, "direct")
+    x_start(0)
+    x_start(1)
+    over(start, 1, 1)
     over(start, 1, 2)
-    over(start, 1, 1)
+    loop(x_traces, 2)
+    x_start(2)
 
     def y_faces(a, values, send, up_buf, down_buf):
         down, up = traces(values)
@@ -402,6 +383,7 @@
     over(start, 0, 1)
     loop(lambda a: z_faces(a, [first[a, :, e] for e in range(MODES)], zs))
     over(start, 0, 2)
+    x_start(3)
 
     def x_own(b):
         values = [first[a, b] for a in range(MODES)]
@@ -421,6 +403,17 @@
     loop(x_own)
     loop(y_own)
     loop(z_own)
+    for axis in range(3):
+        over(receive, 1, axis)
+    orders_edge = jnp.where(lane[0] == cells_z - 1, order_z[1], order_z[0])
+    for side in range(2):
+        pack[side, 1 : cells_y + 1] = orders
+        pack[side, 0:1] = order_y[1]
+        pack[side, cells_y + 1 : cells_y + 2] = order_y[0]
+        pack[side, tall : tall + cells_y] = orders_edge
+        pack[side, 2 * tall : 2 * tall + cells_y] = order_x[side]
+    over(start, 2, 0)
+    x_start(4)
     over(receive, 0, 2)
 
     def z_flux(a):
@@ -429,6 +422,8 @@
             acc[a, :, e] += term(e)
 
     loop(z_flux)
+    x_start(5)
+    forward(0)
     over(receive, 0, 1)
 
     def y_flux(a):
@@ -441,73 +436,8 @@
             coef[a, b] = scale * (-STEP)
 
     loop(y_flux)
-
-    for axis in range(3):
-        over(receive, 1, axis)
-    order_tile[1 : cells_y + 1] = orders
-    order_tile[0:1] = order_y[1]
-    order_tile[cells_y + 1 : cells_y + 2] = order_y[0]
-    for number in late:
-        forward(number)
-    for number in early:
-        x_receive(number)
-
-    def update(a, b, low, high, term):
-        part = slice(low, high)
-        smooth[a, b, part] = acc[a, b, part] + coef[a, b, part] * term(a)
-
-    def x_terms(b, low, high):
-        part = slice(low, high)
-        return face_terms(
-            [xr[0, b, kind, part] for kind in range(2)], [xr[1, b, kind, part] for kind in range(2)]
-        )
-
-    for b in range(2):
-        term = x_terms(b, 0, MODES)
-        for a in range(2):
-            update(a, b, 0, MODES, term)
-        term = x_terms(b, 0, 2)
-        for a in range(2, MODES):
-            update(a, b, 0, 2, term)
-    for b in range(2, MODES):
-        term = x_terms(b, 0, 2)
-        for a in range(2):
-            update(a, b, 0, 2, term)
-
-    centre, edge, x_low, x_high, y_low, y_high = {}, {}, {}, {}, {}, {}
-    edge_orders = jnp.where(lane[0] == cells_z - 1, order_z[1], order_z[0])
-    for key in OCTET:
-        centre[key] = rhs[key]
-    for b in range(2):
-        values = [smooth[a, b, 0:2] for a in range(MODES)]
-        down, up = traces(values)
-        for a in range(2):
-            own = own_row(a, values)
-            below, above = one_sided(down, a, False), one_sided(up, a, True)
-            for e in range(2):
-                centre[a, b, e] = centre[a, b, e] - own[e]
-                x_low[a, b, e] = jnp.where(order_x[1] >= max(a, b, e), -below[e], 0.0)
-                x_high[a, b, e] = jnp.where(order_x[0] >= max(a, b, e), -above[e], 0.0)
-    for a in range(2):
-        values = [smooth[a, b, 0:2] for b in range(MODES)]
-        down, up = traces(values)
-        for b in range(2):
-            own = own_row(b, values)
-            below, above = one_sided(down, b, False), one_sided(up, b, True)
-            for e in range(2):
-                centre[a, b, e] = centre[a, b, e] - own[e]
-                y_low[a, b, e], y_high[a, b, e] = below[e], above[e]
-        values = [smooth[a, 0:2, e] for e in range(MODES)]
-        down, up = traces(values)
-        for e in range(2):
-            below = pltpu.roll(one_sided(down, e, False), cells_z - 1, 2)
-            above = pltpu.roll(one_sided(up, e, True), 1, 2)
-            inner = jnp.where(lane == cells_z - 1, 0.0, below) + jnp.where(lane == 0, 0.0, above)
-            outer = jnp.where(lane == cells_z - 1, below, jnp.where(lane == 0, above, 0.0))
-            own = own_row(e, values) + inner
-            for b in range(2):
-                centre[a, b, e] = centre[a, b, e] - own[b]
-                edge[a, b, e] = jnp.where(edge_orders >= max(a, b, e), -outer[b], 0.0)
+    x_start(6)
+    forward(1)
 
     slots = iter(range(pads.shape[0]))
 
@@ -516,71 +446,130 @@
         pads[slot, at : at + cells_y, :] = value
         return pads[slot]
 
-    own_tile = order_tile[...]
-    resid = {}
-    for key in OCTET:
-        total = padded(centre[key], 1) - padded(y_low[key], 0) - padded(y_high[key], 2)
-        resid[key] = jnp.where(own_tile >= max(key), total, 0.0)
-    resid = corners(resid)
-    near = {key: (corners(x_low)[key], corners(x_high)[key]) for key in OCTET}
-    edge = corners(edge)
+    near, border, layers = {}, {}, {}
+
+    def gather_into(where_to, key, value):
+        where_to[key] = where_to[key] + value if key in where_to else value
+
+    def spread(values, shift, forced, tile_orders, low_orders, high_orders, edge_orders):
+        centre, edge, x_low, x_high, y_low, y_high = {}, {}, {}, {}, {}, {}
+        for b in range(2):
+            line = [values[a, b, 0:2] for a in range(MODES)]
+            down, up = traces(line)
+            for a in range(2):
+                own = own_row(a, line)
+                below, above = one_sided(down, a, False), one_sided(up, a, True)
+                for e in range(2):
+                    centre[a, b, e] = forced[a, b, e] - own[e] if forced is not None else -own[e]
+                    x_low[a, b, e] = jnp.where(low_orders >= max(a, b, e), -below[e], 0.0)
+                    x_high[a, b, e] = jnp.where(high_orders >= max(a, b, e), -above[e], 0.0)
+        for a in range(2):
+            line = [values[a, b, 0:2] for b in range(MODES)]
+            down, up = traces(line)
+            for b in range(2):
+                own = own_row(b, line)
+                below, above = one_sided(down, b, False), one_sided(up, b, True)
+                for e in range(2):
+                    centre[a, b, e] = centre[a, b, e] - own[e]
+                    y_low[a, b, e], y_high[a, b, e] = below[e], above[e]
+            line = [values[a, 0:2, e] for e in range(MODES)]
+            down, up = traces(line)
+            for e in range(2):
+                below = pltpu.roll(one_sided(down, e, False), cells_z - 1, 2)
+                above = pltpu.roll(one_sided(up, e, True), 1, 2)
+                inner = jnp.where(lane == cells_z - 1, 0.0, below) + jnp.where(lane == 0, 0.0, above)
+                outer = jnp.where(lane == cells_z - 1, below, jnp.where(lane == 0, above, 0.0))
+                own = own_row(e, line) + inner
+                for b in range(2):
+                    centre[a, b, e] = centre[a, b, e] - own[b]
+                    edge[a, b, e] = jnp.where(edge_orders >= max(a, b, e), -outer[b], 0.0)
+        resid = {}
+        for key in OCTET:
+            total = padded(centre[key], 1) - padded(y_low[key], 0) - padded(y_high[key], 2)
+            resid[key] = jnp.where(tile_orders >= max(key), total, 0.0)
+        resid, edge, x_low, x_high = corners(resid), corners(edge), corners(x_low), corners(x_high)
+        for i, j, k in OCTET:
+            moved = pltpu.roll(resid[i, j, k], 1, 0) if j else resid[i, j, k]
+            gather_into(layers, (shift + i, k), moved)
+            gather_into(border, (shift + i, j, k), edge[i, j, k])
+            gather_into(near, (shift - 1 + i, j, k), x_low[i, j, k])
+            gather_into(near, (shift + 1 + i, j, k), x_high[i, j, k])
+
+    def ghost(values, side, other_orders):
+        def put(a, b, high):
+            part = slice(0, high)
+            data = [xs[side, b, kind, part] for kind in range(2)]
+            modes = jnp.maximum(last_mode[part], max(a, b))
+            scale = jnp.where(modes <= other_orders[None], table_ref[a, b, part], 0.0) * (-STEP)
+            values[a, b, part] = scale * one_sided(data, a, side == 1)
+
+        for b in range(2):
+            for a in range(MODES):
+                put(a, b, MODES if a < 2 else 2)
+        for b in range(2, MODES):
+            for a in range(2):
+                put(a, b, 2)
+
+    spread(acc, 0, rhs, pack[0, 0:tall], order_x[1], order_x[0], orders_edge)
+    ghost(first, 1, order_x[0])
+    ghost(smooth, 0, order_x[1])
+    forward(2)
+    over(receive, 2, 0)
+    far = slice(2 * tall, 2 * tall + cells_y)
+    rim = slice(tall, tall + cells_y)
+    spread(first, 1, None, pack_in[0, 0:tall], orders, pack_in[0, far], pack_in[0, rim])
+    spread(smooth, -1, None, pack_in[1, 0:tall], pack_in[1, far], orders, pack_in[1, rim])
+
     row_lane = lane[0]
     sums = {}
-    for dx in range(-1, 3):
-        layers = []
+    for dx in REACH:
+        pair = []
         for k in range(2):
-            parts = []
-            if dx in (0, 1):
-                parts += [resid[dx, 0, k], pltpu.roll(resid[dx, 1, k], 1, 0)]
-            for side, i in ((0, dx + 1), (1, dx - 1)):
-                if i in (0, 1):
-                    parts += [padded(near[i, j, k][side], 1 + j) for j in range(2)]
-            layers.append(functools.reduce(lambda p, q: p + q, parts))
-        moved = pltpu.roll(layers[1], 1, 1)
-        if dx in (0, 1):
-            outer = [padded(edge[dx, 0, k], 1) + padded(edge[dx, 1, k], 2) for k in range(2)]
+            parts = [layers[dx, k]] if (dx, k) in layers else []
+            parts += [padded(near[dx, j, k], 1 + j) for j in range(2)]
+            pair.append(functools.reduce(lambda p, q: p + q, parts))
+        moved = pltpu.roll(pair[1], 1, 1)
+        if (dx, 0, 0) in border:
+            outer = [padded(border[dx, 0, k], 1) + padded(border[dx, 1, k], 2) for k in range(2)]
             outer_moved = pltpu.roll(outer[1], 1, 1)
-            inside = layers[0] + jnp.where(row_lane == 0, outer_moved, moved)
+            inside = pair[0] + jnp.where(row_lane == 0, outer_moved, moved)
             beyond = jnp.where(row_lane == 0, moved, outer_moved) + outer[0]
         else:
-            inside = layers[0] + jnp.where(row_lane == 0, 0.0, moved)
+            inside = pair[0] + jnp.where(row_lane == 0, 0.0, moved)
             beyond = jnp.where(row_lane == 0, moved, 0.0)
         for part, value in enumerate((inside, beyond)):
             if dx == 0:
                 sums[part] = value[1 : cells_y + 1]
             else:
-                out_mid[dx + 1, part] = value[1 : cells_y + 1]
-            out_high[dx + 1, part] = value[cells_y + 1 : cells_y + 3]
-            if dx in (0, 1):
-                out_low[dx, part] = value[0:1]
+                out_mid[dx + 2, part] = value[1 : cells_y + 1]
+            out_high[dx + 2, part] = value[cells_y + 1 : cells_y + 3]
+            if -1 <= dx <= 2:
+                out_low[dx + 1, part] = value[0:1]
 
     for number, entry in enumerate(carries):
-        start(entry, 12 + number, *carry_refs(*entry[4:]))
-
-    def late_flux(b):
-        x_receive(b - 2 + len(FIRST_CHUNKS))
-        term = x_terms(b, 2, MODES)
-        for a in range(2):
-            update(a, b, 2, MODES, term)
-        term = x_terms(b, 0, MODES)
-        for a in range(2, MODES):
-            update(a, b, 0, MODES, term)
-
-    for b in range(2):
-        term = x_terms(b, 2, MODES)
-        for a in range(2, MODES):
-            update(a, b, 2, MODES, term)
-    loop(late_flux, 2)
+        start(entry, 14 + number, *carry_refs(*entry[4:]))
+    forward(3)
+
+    def x_flux(b):
+        x_receive(b)
+        term = face_terms(
+            [xr[0, b, kind] for kind in range(2)], [xr[1, b, kind] for kind in range(2)]
+        )
+        for a in range(MODES):
+            smooth[a, b] = acc[a, b] + coef[a, b] * term(a)
+
+    loop(x_flux, RELAYED)
 
     for number, entry in enumerate(carries):
-        receive(entry, 12 + number, *carry_refs(*entry[4:]))
+        receive(entry, 14 + number, *carry_refs(*entry[4:]))
 
     for part in range(2):
         value = sums[part]
-        for at in (0, 2, 3):
-            value = value + in_mid[at, part]
-        high = in_high[0, part] + in_high[1, part] + in_high[2, part] + in_high[3, part]
-        low = in_low[0, part] + in_low[1, part]
+        for dx in REACH:
+            if dx:
+                value = value + in_mid[dx + 2, part]
+        high = functools.reduce(lambda p, q: p + q, [in_high[at, part] for at in range(6)])
+        low = functools.reduce(lambda p, q: p + q, [in_low[at, part] for at in range(4)])
         column[pl.ds(z, 1), part] = value[None]
         column[pl.ds(z, 1), part, 0:2] += high[None]
         column[pl.ds(z, 1), part, cells_y - 1 : cells_y] += low[None]
@@ -588,10 +577,11 @@
     def gather(number, arriving):
         entry = columns[number]
         at = entry[4] if arriving else z
-        return remote(column.at[at], column.at[at], 12 + len(carries) + number, entry[0])
+        return remote(column.at[at], column.at[at], 14 + len(carries) + number, entry[0])
 
     for number in range(len(columns)):
         gather(number, False).start()
+    loop(x_flux, 0, RELAYED)
     for number in range(len(columns)):
         gather(number, True).wait_recv()
 
@@ -608,26 +598,26 @@
             inside = inside & (spot > 0)
         coarse_ref[0, :, zz * cells_z : (zz + 1) * cells_z] = jnp.where(inside, total, 0.0)
 
-    for stage in range(2):
-        for axis in range(3):
+    for stage in range(3):
+        for axis in range(len(stages[stage])):
             if (stage, axis) != (0, 0):
                 over(finish, stage, axis)
-    for number in range(CHUNKS):
+    for b in range(MODES):
         for side in range(2):
 
             @pl.when(halos[side][1])
             def _():
-                x_copy(side, number, halos[side][0]).wait_send()
-
-    for number in late:
+                x_copy(side, b, halos[side][0]).wait_send()
+
+    for b in range(RELAYED):
         for side in range(2):
 
             @pl.when(relays[side][3])
             def _():
-                from_relay(side, number, relays[side][4]).wait_send()
+                from_relay(side, b, relays[side][4]).wait_send()
 
     for number, entry in enumerate(carries):
-        finish(entry, 12 + number, *carry_refs(*entry[4:]))
+        finish(entry, 14 + number, *carry_refs(*entry[4:]))
     for number in range(len(columns)):
         gather(number, False).wait_send()
 
@@ -664,7 +654,7 @@
     def whole(*shape):
         return pltpu.VMEM(shape, jnp.int32)
 
-    slots = 12 + 9 + nz - 1
+    slots = 14 + len(CARRIES) + nz - 1
     coarse_shape = (1, cells_y, nz * cells_z)
     vmem = pl.BlockSpec(memory_space=pltpu.VMEM)
     hbm = pl.BlockSpec(memory_space=pltpu.HBM)
@@ -681,18 +671,18 @@
             buf(*line, *cells), buf(*line, *cells),
             buf(2, MODES, MODES, rows, cells_z), buf(2, MODES, MODES, rows, cells_z),
             whole(2, 1, cells_z), whole(2, *cells), whole(2, 1, cells_z), whole(2, *cells),
-            whole(tall, cells_z), buf(48, tall, cells_z),
-            buf(4, 2, *cells), buf(4, 2, 2, cells_z), buf(2, 2, 1, cells_z),
-            buf(4, 2, *cells), buf(4, 2, 2, cells_z), buf(2, 2, 1, cells_z),
+            whole(2, 3 * tall, cells_z), whole(2, 3 * tall, cells_z), buf(112, tall, cells_z),
+            buf(6, 2, *cells), buf(6, 2, 2, cells_z), buf(4, 2, 1, cells_z),
+            buf(6, 2, *cells), buf(6, 2, 2, cells_z), buf(4, 2, 1, cells_z),
             buf(nz, 2, *cells),
-            buf(2, LATE, 2, LATE, *cells),
+            buf(2, RELAYED, 2, MODES, *cells),
             pltpu.SemaphoreType.DMA((MODES + 2,)),
             pltpu.SemaphoreType.DMA((slots,)),
             pltpu.SemaphoreType.DMA((slots,)),
-            pltpu.SemaphoreType.DMA((2, CHUNKS)),
-            pltpu.SemaphoreType.DMA((2, CHUNKS)),
-            pltpu.SemaphoreType.DMA((2, LATE)),
-            pltpu.SemaphoreType.DMA((2, LATE)),
+            pltpu.SemaphoreType.DMA((2, MODES)),
+            pltpu.SemaphoreType.DMA((2, MODES)),
+            pltpu.SemaphoreType.DMA((2, RELAYED)),
+            pltpu.SemaphoreType.DMA((2, RELAYED)),
         ],
         compiler_params=pltpu.CompilerParams(collective_id=0, has_side_effects=True),
         name="smoother",

time: 17.5 us -> 17.7 us (1.011)
  Pallas kernels: 16.7 us -> 17 us
    pallas_call x1, Pallas kernels: 15.8 us -> 16 us  [per_device(): pl.pallas_call(functools.partial(kernel, sizes, cells_y, cells_z), out_sh...]
where the time goes in v2:
time: 17.7 us; the launch traced here: 17.6 us
  Pallas kernels  17 us (96%)
  between operations  0.64 us (4%)
    pallas_call x1, Pallas kernels, per_device(): pl.pallas_call(functools.partial(kernel, sizes, cells_y, cells_z), out_sh...  16 us
    pallas_call x1, Pallas kernels, per_device(): pl.pallas_call(drain, out_shape=(jax.ShapeDtypeStruct(field.shape, jnp.fl...  0.91 us

profile of v2, /device:TPU:3, one launch (start us, length us, event | category | flops | bytes accessed | tf_op | source)
XLA Modules:
  0.0 17.6 jit_solution(9075202842008036030)
XLA Ops:
  0.6 16.0 %smoother.1 = (f32[7,7,7,4,128]{4,3,2,1,0:T(4,128)S(1)}, f32[1,4,256]{2,1,0:T(4,128)S(1)}) custom-call(f32[7,7,7,4,128]{4,3,2,1,0:T(4,128)} %bitcast.4, s32[1,4,128]{2,1,0:T(4,128)} %orders_hbm.1, f32[7,7,7,1,128]{4,3,2,1,0:T(1,128)} %constant.2.clone.table_hbm), custom_call_target="tpu_custom_call" | custom-call | tf_op jit(solution)/shard_map/smoother/pallas_call | solution.py:661
  16.7 0.9 %drain.1 = (f32[7,7,7,4,128]{4,3,2,1,0:T(4,128)}, f32[1,4,256]{2,1,0:T(4,128)}) custom-call(f32[7,7,7,4,128]{4,3,2,1,0:T(4,128)S(1)} %get-tuple-element.6.smooth, f32[1,4,256]{2,1,0:T(4,128)S(1)} %get-tuple-element.7.coarse), custom_call_target="tpu_custom_call" | custom-call | tf_op jit(solution)/shard_map/drain/pallas_call | solution.py:690

commit v3 on v2

--- a/solution.py
+++ b/solution.py
@@ -111,6 +111,13 @@
 
 OCTET = [(a, b, e) for a in range(2) for b in range(2) for e in range(2)]
 RELAYED = 4
+SIGNS = (1, -1)
+DIAGONALS = (
+    [(dx, dy, 0) for dx in SIGNS for dy in SIGNS]
+    + [(dx, 0, dz) for dx in SIGNS for dz in SIGNS]
+    + [(2 * dx, 0, 0) for dx in SIGNS]
+)
+Y_PARTS = ((slice(0, 2), slice(0, MODES)), (slice(2, MODES), slice(0, 2)), (slice(2, MODES), slice(2, MODES)))
 REACH = range(-2, 4)
 CARRIES = (
     (3, 1), (2, 1), (-2, 1), (1, 1), (-1, 1), (2, -1), (1, -1), (-1, -1),
@@ -120,11 +127,11 @@
 
 def kernel(
     sizes, cells_y, cells_z, rhs_hbm, orders_hbm, table_hbm, smooth, coarse_ref,
-    rhs, first, acc, coef, orders_ref, table_ref,
+    rhs, first, acc, coef, lead, ghost_up, ghost_down, orders_ref, table_ref,
     xs, xr, ys, yr, zs, zr, y_up, y_down,
-    order_line, order_x, order_y, order_z, pack, pack_in, pads,
+    order_line, order_x, order_y, order_z, order_xy, order_xz, order_far, order_tile, pads,
     out_mid, out_high, out_low, in_mid, in_high, in_low, column,
-    relay, local_sem, send_sem, recv_sem, x_send, x_recv, relay_in, relay_out,
+    relay, local_sem, send_sem, recv_sem, x_send, x_recv, y_send, y_recv, relay_in, relay_out,
 ):
     nx, ny, nz = sizes
     tall = pads.shape[1]
@@ -158,6 +165,29 @@
         source = lax.rem(z - r + nz, nz)
         columns.append(((x, y, lax.rem(z + r, nz)), always, (x, y, source), always, source))
 
+    def diagonal(offset):
+        here = (x, y, z)
+        to = tuple(h + d for h, d in zip(here, offset))
+        back = tuple(h - d for h, d in zip(here, offset))
+        ok_to, ok_from = always, always
+        for axis, d in enumerate(offset):
+            low, high = here[axis] >= abs(d), here[axis] + abs(d) < sizes[axis]
+            if d > 0:
+                ok_to, ok_from = ok_to & high, ok_from & low
+            elif d < 0:
+                ok_to, ok_from = ok_to & low, ok_from & high
+        return (to, ok_to, back, ok_from)
+
+    diagonals = [diagonal(offset) for offset in DIAGONALS]
+
+    def diagonal_refs(offset):
+        dx, dy, dz = offset
+        if dy:
+            return order_line.at[0 if dy < 0 else 1], order_xy.at[(1 + dx) // 2, (1 + dy) // 2]
+        if dz:
+            return orders_ref.at[0], order_xz.at[(1 + dx) // 2, (1 + dz) // 2]
+        return orders_ref.at[0], order_far.at[(2 + dx) // 4]
+
     odd = lax.rem(x, 2) == 1
     even = jnp.logical_not(odd)
     relays = (
@@ -166,7 +196,7 @@
     )
 
     expected = jnp.int32(0)
-    for entry in halos[:4] + columns + list(relays) + carries[:1]:
+    for entry in halos[:4] + columns + diagonals + carries[:1]:
         to, ok_to, back, ok_from = entry[:4]
 
         @pl.when(ok_from)
@@ -189,6 +219,11 @@
         rhs_load(b).start()
 
     def remote(src, dst, slot, to):
+        if isinstance(slot, tuple):
+            return pltpu.make_async_remote_copy(
+                src_ref=src, dst_ref=dst, send_sem=y_send.at[slot], recv_sem=y_recv.at[slot],
+                device_id=to, device_id_type=MESH,
+            )
         return pltpu.make_async_remote_copy(
             src_ref=src, dst_ref=dst, send_sem=send_sem.at[slot], recv_sem=recv_sem.at[slot],
             device_id=to, device_id_type=MESH,
@@ -218,7 +253,6 @@
     stages = (
         ((xs, xr), (ys, yr), (zs, zr)),
         ((orders_ref, order_x), (order_line, order_y), (orders_ref, order_z)),
-        ((pack, pack_in),),
     )
 
     def over(action, stage, axis):
@@ -227,8 +261,8 @@
             index = 2 * axis + side
             action(halos[index], 6 * stage + index, src.at[0 if src is orders_ref else side], dst.at[side])
 
-    for stage, empty in ((0, 0.0), (1, -1), (2, -1)):
-        for axis in range(len(stages[stage])):
+    for stage, empty in ((0, 0.0), (1, -1)):
+        for axis in range(3):
             for side in range(2):
                 dst = stages[stage][axis][1]
 
@@ -237,7 +271,14 @@
                     dst[side] = jnp.full(dst.shape[1:], empty, dst.dtype)
 
     pads[...] = jnp.zeros(pads.shape, jnp.float32)
-    pack[...] = jnp.full(pack.shape, -1, jnp.int32)
+    order_tile[...] = jnp.full(order_tile.shape, -1, jnp.int32)
+    for offset, entry in zip(DIAGONALS, diagonals):
+
+        @pl.when(jnp.logical_not(entry[3]))
+        def _(offset=offset):
+            dst = diagonal_refs(offset)[1]
+            dst[...] = jnp.full(dst.shape, -1, jnp.int32)
+
     targets = {0: (out_mid, in_mid), 1: (out_high, in_high), -1: (out_low, in_low)}
 
     def carry_refs(dx, dy):
@@ -336,15 +377,25 @@
             def _():
                 x_copy(side, b, to).start()
 
+    def diagonal_over(action):
+        for number, (offset, entry) in enumerate(zip(DIAGONALS, diagonals)):
+            action(entry, 14 + number, *diagonal_refs(offset))
+
+    def y_over(action, part):
+        modes = Y_PARTS[part]
+        for side in range(2):
+            at = (side, slice(None)) + modes
+            action(halos[2 + side], (side, part), ys.at[at], yr.at[at])
+
     loop(x_traces, 0, 2)
     pl.semaphore_wait(barrier, expected)
     over(start, 1, 0)
+    diagonal_over(start)
     x_start(0)
     x_start(1)
     over(start, 1, 1)
     over(start, 1, 2)
     loop(x_traces, 2)
-    x_start(2)
 
     def y_faces(a, values, send, up_buf, down_buf):
         down, up = traces(values)
@@ -354,13 +405,13 @@
             send[0, kind, a] = down[kind][:, 0:1, :]
             send[1, kind, a] = up[kind][:, cells_y - 1 : cells_y, :]
 
-    def y_neighbours(a, received, up_buf, down_buf):
+    def y_neighbours(a, received, up_buf, down_buf, part=slice(0, MODES)):
         for kind in range(2):
-            up_buf[kind, a, :, cells_y : cells_y + 1, :] = received[0, kind, a]
-            down_buf[kind, a, :, 0:1, :] = received[1, kind, a]
-        return face_terms(
-            [up_buf[kind, a, :, 1 : cells_y + 1, :] for kind in range(2)],
-            [down_buf[kind, a, :, 0:cells_y, :] for kind in range(2)],
+            up_buf[kind, a, part, cells_y : cells_y + 1, :] = received[0, kind, a, part]
+            down_buf[kind, a, part, 0:1, :] = received[1, kind, a, part]
+        return (
+            [up_buf[kind, a, part, 1 : cells_y + 1, :] for kind in range(2)],
+            [down_buf[kind, a, part, 0:cells_y, :] for kind in range(2)],
         )
 
     def z_faces(a, values, send):
@@ -369,75 +420,96 @@
             for kind in range(2):
                 send[side, kind, a] = sides[side][kind]
 
-    def z_neighbours(a, send, received):
+    def z_neighbours(a, send, received, part=slice(0, MODES)):
         def moved(side, kind, edge, amount):
-            picked = jnp.where(lane == edge, received[side, kind, a], send[side, kind, a])
+            picked = jnp.where(lane == edge, received[side, kind, a, part], send[side, kind, a, part])
             return pltpu.roll(picked, amount, 2)
 
-        return face_terms(
+        return (
             [moved(0, kind, 0, cells_z - 1) for kind in range(2)],
             [moved(1, kind, cells_z - 1, 1) for kind in range(2)],
         )
 
-    loop(lambda a: y_faces(a, [first[a, b] for b in range(MODES)], ys, y_up, y_down))
-    over(start, 0, 1)
+    def narrow(pair):
+        return [[value[0:2] for value in side] for side in pair]
+
+    def y_traces(a):
+        y_faces(a, [first[a, b] for b in range(MODES)], ys, y_up, y_down)
+
+    loop(y_traces, 0, 2)
+    y_over(start, 0)
+    loop(y_traces, 2)
+    y_over(start, 1)
+    y_over(start, 2)
+    x_start(2)
     loop(lambda a: z_faces(a, [first[a, :, e] for e in range(MODES)], zs))
     over(start, 0, 2)
     x_start(3)
 
-    def x_own(b):
+    few = slice(0, 2)
+
+    def predict(a, b, part, total):
+        right = rhs[a, b, part]
+        modes = jnp.maximum(last_mode[part], jnp.maximum(a, b))
+        scale = jnp.where(modes <= orders[None], table_ref[a, b, part], 0.0)
+        return scale * (KEEP * right + STEP * (right - total)), scale * (-STEP)
+
+    for b in range(2):
         values = [first[a, b] for a in range(MODES)]
-        for a in range(MODES):
-            acc[a, b] = own_row(a, values)
-
-    def y_own(a):
+        for a in range(2):
+            lead[a, b] = own_row(a, values)
+        values = [value[0:2] for value in values]
+        for a in range(2, MODES):
+            lead[a, b, few] = own_row(a, values)
+
+    def lead_x(b):
+        values = [first[a, b, few] for a in range(MODES)]
+        for a in range(2):
+            lead[a, b, few] = own_row(a, values)
+
+    def lead_y(a):
+        values = [first[a, b, few] for b in range(MODES)]
+        for b in range(2):
+            lead[a, b, few] += own_row(b, values)
+
+    def lead_z(a):
+        values = [first[a, few, e] for e in range(MODES)]
+        for e in range(2):
+            lead[a, few, e] += own_row(e, values)
+
+    loop(lead_x, 2)
+    for a in range(2):
         values = [first[a, b] for b in range(MODES)]
-        for b in range(MODES):
-            acc[a, b] += own_row(b, values)
-
-    def z_own(a):
+        for b in range(2):
+            lead[a, b] += own_row(b, values)
+        values = [value[0:2] for value in values]
+        for b in range(2, MODES):
+            lead[a, b, few] += own_row(b, values)
+    loop(lead_y, 2)
+    for a in range(2):
         values = [first[a, :, e] for e in range(MODES)]
-        for e in range(MODES):
-            acc[a, :, e] += own_row(e, values)
-
-    loop(x_own)
-    loop(y_own)
-    loop(z_own)
-    for axis in range(3):
-        over(receive, 1, axis)
-    orders_edge = jnp.where(lane[0] == cells_z - 1, order_z[1], order_z[0])
-    for side in range(2):
-        pack[side, 1 : cells_y + 1] = orders
-        pack[side, 0:1] = order_y[1]
-        pack[side, cells_y + 1 : cells_y + 2] = order_y[0]
-        pack[side, tall : tall + cells_y] = orders_edge
-        pack[side, 2 * tall : 2 * tall + cells_y] = order_x[side]
-    over(start, 2, 0)
-    x_start(4)
+        for e in range(2):
+            lead[a, :, e] += own_row(e, values)
+        values = [value[0:2] for value in values]
+        for e in range(2, MODES):
+            lead[a, few, e] += own_row(e, values)
+    loop(lead_z, 2)
     over(receive, 0, 2)
 
-    def z_flux(a):
-        term = z_neighbours(a, zs, zr)
-        for e in range(MODES):
-            acc[a, :, e] += term(e)
-
-    loop(z_flux)
-    x_start(5)
-    forward(0)
-    over(receive, 0, 1)
-
-    def y_flux(a):
-        term = y_neighbours(a, yr, y_up, y_down)
-        for b in range(MODES):
-            right = rhs[a, b]
-            total = acc[a, b] + term(b)
-            scale = jnp.where(active(a, b), table_ref[a, b], 0.0)
-            acc[a, b] = scale * (KEEP * right + STEP * (right - total))
-            coef[a, b] = scale * (-STEP)
-
-    loop(y_flux)
-    x_start(6)
-    forward(1)
+    def lead_z_flux(a):
+        term = face_terms(*z_neighbours(a, zs, zr, few))
+        for e in range(2):
+            lead[a, few, e] += term(e)
+
+    for a in range(2):
+        pair = z_neighbours(a, zs, zr)
+        term = face_terms(*pair)
+        for e in range(2):
+            lead[a, :, e] += term(e)
+        term = face_terms(*narrow(pair))
+        for e in range(2, MODES):
+            lead[a, few, e] += term(e)
+    loop(lead_z_flux, 2)
 
     slots = iter(range(pads.shape[0]))
 
@@ -510,15 +582,42 @@
             for a in range(2):
                 put(a, b, 2)
 
-    spread(acc, 0, rhs, pack[0, 0:tall], order_x[1], order_x[0], orders_edge)
-    ghost(first, 1, order_x[0])
-    ghost(smooth, 0, order_x[1])
-    forward(2)
-    over(receive, 2, 0)
-    far = slice(2 * tall, 2 * tall + cells_y)
-    rim = slice(tall, tall + cells_y)
-    spread(first, 1, None, pack_in[0, 0:tall], orders, pack_in[0, far], pack_in[0, rim])
-    spread(smooth, -1, None, pack_in[1, 0:tall], pack_in[1, far], orders, pack_in[1, rim])
+    for axis in range(3):
+        over(receive, 1, axis)
+    diagonal_over(receive)
+    edges = []
+    rows_of = (orders, order_x[0], order_x[1])
+    lines_of = (order_y, order_xy.at[0], order_xy.at[1])
+    sides_of = (order_z, order_xz.at[0], order_xz.at[1])
+    for at in range(3):
+        order_tile[at, 1 : cells_y + 1] = rows_of[at]
+        order_tile[at, 0:1] = lines_of[at][1]
+        order_tile[at, cells_y + 1 : cells_y + 2] = lines_of[at][0]
+        edges.append(jnp.where(lane[0] == cells_z - 1, sides_of[at][1], sides_of[at][0]))
+    ghost(ghost_up, 1, order_x[0])
+    ghost(ghost_down, 0, order_x[1])
+    spread(ghost_up, 1, None, order_tile[1], orders, order_far[0], edges[1])
+    x_start(4)
+    spread(ghost_down, -1, None, order_tile[2], order_far[1], orders, edges[2])
+    forward(0)
+    y_over(receive, 0)
+    y_over(receive, 1)
+
+    def lead_y_flux(a):
+        term = face_terms(*y_neighbours(a, yr, y_up, y_down, few))
+        for b in range(2):
+            lead[a, b, few] = predict(a, b, few, lead[a, b, few] + term(b))[0]
+
+    for a in range(2):
+        pair = y_neighbours(a, yr, y_up, y_down)
+        term = face_terms(*pair)
+        for b in range(2):
+            lead[a, b] = predict(a, b, slice(0, MODES), lead[a, b] + term(b))[0]
+        term = face_terms(*narrow(pair))
+        for b in range(2, MODES):
+            lead[a, b, few] = predict(a, b, few, lead[a, b, few] + term(b))[0]
+    loop(lead_y_flux, 2)
+    spread(lead, 0, rhs, order_tile[0], order_x[1], order_x[0], edges[0])
 
     row_lane = lane[0]
     sums = {}
@@ -547,8 +646,44 @@
                 out_low[dx + 1, part] = value[0:1]
 
     for number, entry in enumerate(carries):
-        start(entry, 14 + number, *carry_refs(*entry[4:]))
+        start(entry, 24 + number, *carry_refs(*entry[4:]))
+    x_start(5)
+    forward(1)
+
+    def x_own(b):
+        values = [first[a, b] for a in range(MODES)]
+        for a in range(MODES):
+            acc[a, b] = own_row(a, values)
+
+    def y_own(a):
+        values = [first[a, b] for b in range(MODES)]
+        for b in range(MODES):
+            acc[a, b] += own_row(b, values)
+
+    def z_own(a):
+        values = [first[a, :, e] for e in range(MODES)]
+        for e in range(MODES):
+            acc[a, :, e] += own_row(e, values)
+
+    def z_flux(a):
+        term = face_terms(*z_neighbours(a, zs, zr))
+        for e in range(MODES):
+            acc[a, :, e] += term(e)
+
+    def y_flux(a):
+        term = face_terms(*y_neighbours(a, yr, y_up, y_down))
+        for b in range(MODES):
+            acc[a, b], coef[a, b] = predict(a, b, slice(0, MODES), acc[a, b] + term(b))
+
+    loop(x_own)
+    x_start(6)
+    forward(2)
+    loop(y_own)
     forward(3)
+    loop(z_own)
+    loop(z_flux)
+    y_over(receive, 2)
+    loop(y_flux)
 
     def x_flux(b):
         x_receive(b)
@@ -561,7 +696,7 @@
     loop(x_flux, RELAYED)
 
     for number, entry in enumerate(carries):
-        receive(entry, 14 + number, *carry_refs(*entry[4:]))
+        receive(entry, 24 + number, *carry_refs(*entry[4:]))
 
     for part in range(2):
         value = sums[part]
@@ -577,7 +712,7 @@
     def gather(number, arriving):
         entry = columns[number]
         at = entry[4] if arriving else z
-        return remote(column.at[at], column.at[at], 14 + len(carries) + number, entry[0])
+        return remote(column.at[at], column.at[at], 24 + len(carries) + number, entry[0])
 
     for number in range(len(columns)):
         gather(number, False).start()
@@ -598,10 +733,11 @@
             inside = inside & (spot > 0)
         coarse_ref[0, :, zz * cells_z : (zz + 1) * cells_z] = jnp.where(inside, total, 0.0)
 
-    for stage in range(3):
-        for axis in range(len(stages[stage])):
-            if (stage, axis) != (0, 0):
-                over(finish, stage, axis)
+    for stage, axis in ((0, 2), (1, 0), (1, 1), (1, 2)):
+        over(finish, stage, axis)
+    for part in range(3):
+        y_over(finish, part)
+    diagonal_over(finish)
     for b in range(MODES):
         for side in range(2):
 
@@ -617,7 +753,7 @@
                 from_relay(side, b, relays[side][4]).wait_send()
 
     for number, entry in enumerate(carries):
-        finish(entry, 14 + number, *carry_refs(*entry[4:]))
+        finish(entry, 24 + number, *carry_refs(*entry[4:]))
     for number in range(len(columns)):
         gather(number, False).wait_send()
 
@@ -654,7 +790,7 @@
     def whole(*shape):
         return pltpu.VMEM(shape, jnp.int32)
 
-    slots = 14 + len(CARRIES) + nz - 1
+    slots = 24 + len(CARRIES) + nz - 1
     coarse_shape = (1, cells_y, nz * cells_z)
     vmem = pl.BlockSpec(memory_space=pltpu.VMEM)
     hbm = pl.BlockSpec(memory_space=pltpu.HBM)
@@ -663,7 +799,7 @@
         out_shape=(pltpu.VMEM(field.shape, jnp.float32), pltpu.VMEM(coarse_shape, jnp.float32)),
         in_specs=[hbm, hbm, hbm],
         out_specs=(vmem, vmem),
-        scratch_shapes=[buf(*field.shape)] * 4
+        scratch_shapes=[buf(*field.shape)] * 7
         + [
             whole(*orders.shape), buf(*table.shape),
             buf(2, MODES, 2, MODES, *cells), buf(2, MODES, 2, MODES, *cells),
@@ -671,7 +807,8 @@
             buf(*line, *cells), buf(*line, *cells),
             buf(2, MODES, MODES, rows, cells_z), buf(2, MODES, MODES, rows, cells_z),
             whole(2, 1, cells_z), whole(2, *cells), whole(2, 1, cells_z), whole(2, *cells),
-            whole(2, 3 * tall, cells_z), whole(2, 3 * tall, cells_z), buf(112, tall, cells_z),
+            whole(2, 2, 1, cells_z), whole(2, 2, *cells), whole(2, *cells), whole(3, tall, cells_z),
+            buf(112, tall, cells_z),
             buf(6, 2, *cells), buf(6, 2, 2, cells_z), buf(4, 2, 1, cells_z),
             buf(6, 2, *cells), buf(6, 2, 2, cells_z), buf(4, 2, 1, cells_z),
             buf(nz, 2, *cells),
@@ -681,6 +818,8 @@
             pltpu.SemaphoreType.DMA((slots,)),
             pltpu.SemaphoreType.DMA((2, MODES)),
             pltpu.SemaphoreType.DMA((2, MODES)),
+            pltpu.SemaphoreType.DMA((2, 3)),
+            pltpu.SemaphoreType.DMA((2, 3)),
             pltpu.SemaphoreType.DMA((2, RELAYED)),
             pltpu.SemaphoreType.DMA((2, RELAYED)),
         ],

time: 17.7 us -> 17.5 us (0.989)
  the two profiles are of different devices: /device:TPU:3 before, /device:TPU:0 now
where the time goes in v3:
time: 17.5 us; the launch traced here: 17.3 us
  Pallas kernels  16.7 us (95%)
  between operations  0.64 us (4%)
    pallas_call x1, Pallas kernels, per_device(): pl.pallas_call(functools.partial(kernel, sizes, cells_y, cells_z), out_sh...  15.8 us
    pallas_call x1, Pallas kernels, per_device(): pl.pallas_call(drain, out_shape=(jax.ShapeDtypeStruct(field.shape, jnp.fl...  0.91 us

profile of v3, /device:TPU:0, one launch (start us, length us, event | category | flops | bytes accessed | tf_op | source)
XLA Modules:
  0.0 17.3 jit_solution(5109069559010928058)
XLA Ops:
  0.6 15.8 %smoother.1 = (f32[7,7,7,4,128]{4,3,2,1,0:T(4,128)S(1)}, f32[1,4,256]{2,1,0:T(4,128)S(1)}) custom-call(f32[7,7,7,4,128]{4,3,2,1,0:T(4,128)} %bitcast.4, s32[1,4,128]{2,1,0:T(4,128)} %orders_hbm.1, f32[7,7,7,1,128]{4,3,2,1,0:T(1,128)} %constant.2.clone.table_hbm), custom_call_target="tpu_custom_call" | custom-call | tf_op jit(solution)/shard_map/smoother/pallas_call | solution.py:797
  16.4 0.9 %drain.1 = (f32[7,7,7,4,128]{4,3,2,1,0:T(4,128)}, f32[1,4,256]{2,1,0:T(4,128)}) custom-call(f32[7,7,7,4,128]{4,3,2,1,0:T(4,128)S(1)} %get-tuple-element.6.smooth, f32[1,4,256]{2,1,0:T(4,128)S(1)} %get-tuple-element.7.coarse), custom_call_target="tpu_custom_call" | custom-call | tf_op jit(solution)/shard_map/drain/pallas_call | solution.py:829

commit v4 on v3

--- a/solution.py
+++ b/solution.py
@@ -127,11 +127,11 @@
 
 def kernel(
     sizes, cells_y, cells_z, rhs_hbm, orders_hbm, table_hbm, smooth, coarse_ref,
-    rhs, first, acc, coef, lead, ghost_up, ghost_down, orders_ref, table_ref,
+    rhs, first, acc, coef, ghost_up, ghost_down, orders_ref, table_ref,
     xs, xr, ys, yr, zs, zr, y_up, y_down,
     order_line, order_x, order_y, order_z, order_xy, order_xz, order_far, order_tile, pads,
     out_mid, out_high, out_low, in_mid, in_high, in_low, column,
-    relay, local_sem, send_sem, recv_sem, x_send, x_recv, y_send, y_recv, relay_in, relay_out,
+    relay, local_sem, send_sem, recv_sem, x_send, x_recv, y_send, y_recv, relay_in, relay_out, met,
 ):
     nx, ny, nz = sizes
     tall = pads.shape[1]
@@ -196,7 +196,7 @@
     )
 
     expected = jnp.int32(0)
-    for entry in halos[:4] + columns + diagonals + carries[:1]:
+    for entry in halos[:4] + columns + list(relays):
         to, ok_to, back, ok_from = entry[:4]
 
         @pl.when(ok_from)
@@ -387,14 +387,23 @@
             at = (side, slice(None)) + modes
             action(halos[2 + side], (side, part), ys.at[at], yr.at[at])
 
+    def meet(action):
+        for side in range(2):
+            to, ok_to, _, ok_from = halos[side]
+
+            @pl.when(ok_to if action == "tell" else ok_from)
+            def _():
+                if action == "tell":
+                    pl.semaphore_signal(met.at[side], inc=1, device_id=to, device_id_type=MESH)
+                else:
+                    pl.semaphore_wait(met.at[side], 1)
+
     loop(x_traces, 0, 2)
     pl.semaphore_wait(barrier, expected)
+    meet("tell")
     over(start, 1, 0)
-    diagonal_over(start)
     x_start(0)
     x_start(1)
-    over(start, 1, 1)
-    over(start, 1, 2)
     loop(x_traces, 2)
 
     def y_faces(a, values, send, up_buf, down_buf):
@@ -430,9 +439,6 @@
             [moved(1, kind, cells_z - 1, 1) for kind in range(2)],
         )
 
-    def narrow(pair):
-        return [[value[0:2] for value in side] for side in pair]
-
     def y_traces(a):
         y_faces(a, [first[a, b] for b in range(MODES)], ys, y_up, y_down)
 
@@ -440,13 +446,15 @@
     y_over(start, 0)
     loop(y_traces, 2)
     y_over(start, 1)
+    over(start, 1, 1)
+    meet("hear")
+    diagonal_over(start)
+    x_start(2)
+    over(start, 1, 2)
     y_over(start, 2)
-    x_start(2)
     loop(lambda a: z_faces(a, [first[a, :, e] for e in range(MODES)], zs))
     over(start, 0, 2)
     x_start(3)
-
-    few = slice(0, 2)
 
     def predict(a, b, part, total):
         right = rhs[a, b, part]
@@ -454,62 +462,48 @@
         scale = jnp.where(modes <= orders[None], table_ref[a, b, part], 0.0)
         return scale * (KEEP * right + STEP * (right - total)), scale * (-STEP)
 
-    for b in range(2):
+    def x_own(b):
         values = [first[a, b] for a in range(MODES)]
-        for a in range(2):
-            lead[a, b] = own_row(a, values)
-        values = [value[0:2] for value in values]
-        for a in range(2, MODES):
-            lead[a, b, few] = own_row(a, values)
-
-    def lead_x(b):
-        values = [first[a, b, few] for a in range(MODES)]
-        for a in range(2):
-            lead[a, b, few] = own_row(a, values)
-
-    def lead_y(a):
-        values = [first[a, b, few] for b in range(MODES)]
-        for b in range(2):
-            lead[a, b, few] += own_row(b, values)
-
-    def lead_z(a):
-        values = [first[a, few, e] for e in range(MODES)]
-        for e in range(2):
-            lead[a, few, e] += own_row(e, values)
-
-    loop(lead_x, 2)
-    for a in range(2):
+        for a in range(MODES):
+            acc[a, b] = own_row(a, values)
+
+    def y_own(a):
         values = [first[a, b] for b in range(MODES)]
-        for b in range(2):
-            lead[a, b] += own_row(b, values)
-        values = [value[0:2] for value in values]
-        for b in range(2, MODES):
-            lead[a, b, few] += own_row(b, values)
-    loop(lead_y, 2)
-    for a in range(2):
+        for b in range(MODES):
+            acc[a, b] += own_row(b, values)
+
+    def z_own(a):
         values = [first[a, :, e] for e in range(MODES)]
-        for e in range(2):
-            lead[a, :, e] += own_row(e, values)
-        values = [value[0:2] for value in values]
-        for e in range(2, MODES):
-            lead[a, few, e] += own_row(e, values)
-    loop(lead_z, 2)
+        for e in range(MODES):
+            acc[a, :, e] += own_row(e, values)
+
+    def z_flux(a):
+        term = face_terms(*z_neighbours(a, zs, zr))
+        for e in range(MODES):
+            acc[a, :, e] += term(e)
+
+    def y_flux(a):
+        term = face_terms(*y_neighbours(a, yr, y_up, y_down))
+        for b in range(MODES):
+            acc[a, b], coef[a, b] = predict(a, b, slice(0, MODES), acc[a, b] + term(b))
+
+    def y_flux_part(part):
+        def step(a):
+            term = face_terms(*y_neighbours(a, yr, y_up, y_down, part))
+            for b in range(MODES):
+                acc[a, b, part], coef[a, b, part] = predict(a, b, part, acc[a, b, part] + term(b))
+
+        loop(step, 2)
+
+    loop(x_own)
+    x_start(4)
+    x_start(5)
+    loop(y_own)
+    x_start(6)
+    loop(z_own)
     over(receive, 0, 2)
-
-    def lead_z_flux(a):
-        term = face_terms(*z_neighbours(a, zs, zr, few))
-        for e in range(2):
-            lead[a, few, e] += term(e)
-
-    for a in range(2):
-        pair = z_neighbours(a, zs, zr)
-        term = face_terms(*pair)
-        for e in range(2):
-            lead[a, :, e] += term(e)
-        term = face_terms(*narrow(pair))
-        for e in range(2, MODES):
-            lead[a, few, e] += term(e)
-    loop(lead_z_flux, 2)
+    loop(z_flux)
+    forward(0)
 
     slots = iter(range(pads.shape[0]))
 
@@ -584,40 +578,32 @@
 
     for axis in range(3):
         over(receive, 1, axis)
-    diagonal_over(receive)
-    edges = []
     rows_of = (orders, order_x[0], order_x[1])
     lines_of = (order_y, order_xy.at[0], order_xy.at[1])
     sides_of = (order_z, order_xz.at[0], order_xz.at[1])
-    for at in range(3):
+
+    def surroundings(at):
         order_tile[at, 1 : cells_y + 1] = rows_of[at]
         order_tile[at, 0:1] = lines_of[at][1]
         order_tile[at, cells_y + 1 : cells_y + 2] = lines_of[at][0]
-        edges.append(jnp.where(lane[0] == cells_z - 1, sides_of[at][1], sides_of[at][0]))
+        edge_orders = jnp.where(lane[0] == cells_z - 1, sides_of[at][1], sides_of[at][0])
+        return order_tile[at], edge_orders
+
     ghost(ghost_up, 1, order_x[0])
     ghost(ghost_down, 0, order_x[1])
-    spread(ghost_up, 1, None, order_tile[1], orders, order_far[0], edges[1])
-    x_start(4)
-    spread(ghost_down, -1, None, order_tile[2], order_far[1], orders, edges[2])
-    forward(0)
     y_over(receive, 0)
+    loop(y_flux, 0, 2)
     y_over(receive, 1)
-
-    def lead_y_flux(a):
-        term = face_terms(*y_neighbours(a, yr, y_up, y_down, few))
-        for b in range(2):
-            lead[a, b, few] = predict(a, b, few, lead[a, b, few] + term(b))[0]
-
-    for a in range(2):
-        pair = y_neighbours(a, yr, y_up, y_down)
-        term = face_terms(*pair)
-        for b in range(2):
-            lead[a, b] = predict(a, b, slice(0, MODES), lead[a, b] + term(b))[0]
-        term = face_terms(*narrow(pair))
-        for b in range(2, MODES):
-            lead[a, b, few] = predict(a, b, few, lead[a, b, few] + term(b))[0]
-    loop(lead_y_flux, 2)
-    spread(lead, 0, rhs, order_tile[0], order_x[1], order_x[0], edges[0])
+    y_flux_part(slice(0, 2))
+    forward(1)
+    tile_orders, edge_orders = surroundings(0)
+    spread(acc, 0, rhs, tile_orders, order_x[1], order_x[0], edge_orders)
+    diagonal_over(receive)
+    forward(2)
+    tile_orders, edge_orders = surroundings(1)
+    spread(ghost_up, 1, None, tile_orders, orders, order_far[0], edge_orders)
+    tile_orders, edge_orders = surroundings(2)
+    spread(ghost_down, -1, None, tile_orders, order_far[1], orders, edge_orders)
 
     row_lane = lane[0]
     sums = {}
@@ -647,43 +633,9 @@
 
     for number, entry in enumerate(carries):
         start(entry, 24 + number, *carry_refs(*entry[4:]))
-    x_start(5)
-    forward(1)
-
-    def x_own(b):
-        values = [first[a, b] for a in range(MODES)]
-        for a in range(MODES):
-            acc[a, b] = own_row(a, values)
-
-    def y_own(a):
-        values = [first[a, b] for b in range(MODES)]
-        for b in range(MODES):
-            acc[a, b] += own_row(b, values)
-
-    def z_own(a):
-        values = [first[a, :, e] for e in range(MODES)]
-        for e in range(MODES):
-            acc[a, :, e] += own_row(e, values)
-
-    def z_flux(a):
-        term = face_terms(*z_neighbours(a, zs, zr))
-        for e in range(MODES):
-            acc[a, :, e] += term(e)
-
-    def y_flux(a):
-        term = face_terms(*y_neighbours(a, yr, y_up, y_down))
-        for b in range(MODES):
-            acc[a, b], coef[a, b] = predict(a, b, slice(0, MODES), acc[a, b] + term(b))
-
-    loop(x_own)
-    x_start(6)
-    forward(2)
-    loop(y_own)
     forward(3)
-    loop(z_own)
-    loop(z_flux)
     y_over(receive, 2)
-    loop(y_flux)
+    y_flux_part(slice(2, MODES))
 
     def x_flux(b):
         x_receive(b)
@@ -694,6 +646,25 @@
             smooth[a, b] = acc[a, b] + coef[a, b] * term(a)
 
     loop(x_flux, RELAYED)
+
+    for stage, axis in ((0, 2), (1, 0), (1, 1), (1, 2)):
+        over(finish, stage, axis)
+    for part in range(3):
+        y_over(finish, part)
+    diagonal_over(finish)
+    for b in range(MODES):
+        for side in range(2):
+
+            @pl.when(halos[side][1])
+            def _():
+                x_copy(side, b, halos[side][0]).wait_send()
+
+    for b in range(RELAYED):
+        for side in range(2):
+
+            @pl.when(relays[side][3])
+            def _():
+                from_relay(side, b, relays[side][4]).wait_send()
 
     for number, entry in enumerate(carries):
         receive(entry, 24 + number, *carry_refs(*entry[4:]))
@@ -717,8 +688,12 @@
     for number in range(len(columns)):
         gather(number, False).start()
     loop(x_flux, 0, RELAYED)
+    for number, entry in enumerate(carries):
+        finish(entry, 24 + number, *carry_refs(*entry[4:]))
     for number in range(len(columns)):
         gather(number, True).wait_recv()
+    for number in range(len(columns)):
+        gather(number, False).wait_send()
 
     row = lax.broadcasted_iota(jnp.int32, (cells_y, cells_z), 0)
     spot = lax.broadcasted_iota(jnp.int32, (cells_y, cells_z), 1)
@@ -732,30 +707,6 @@
         if zz == 0:
             inside = inside & (spot > 0)
         coarse_ref[0, :, zz * cells_z : (zz + 1) * cells_z] = jnp.where(inside, total, 0.0)
-
-    for stage, axis in ((0, 2), (1, 0), (1, 1), (1, 2)):
-        over(finish, stage, axis)
-    for part in range(3):
-        y_over(finish, part)
-    diagonal_over(finish)
-    for b in range(MODES):
-        for side in range(2):
-
-            @pl.when(halos[side][1])
-            def _():
-                x_copy(side, b, halos[side][0]).wait_send()
-
-    for b in range(RELAYED):
-        for side in range(2):
-
-            @pl.when(relays[side][3])
-            def _():
-                from_relay(side, b, relays[side][4]).wait_send()
-
-    for number, entry in enumerate(carries):
-        finish(entry, 24 + number, *carry_refs(*entry[4:]))
-    for number in range(len(columns)):
-        gather(number, False).wait_send()
 
 
 def drain(smooth, coarse, smooth_hbm, coarse_hbm, sem):
@@ -799,7 +750,7 @@
         out_shape=(pltpu.VMEM(field.shape, jnp.float32), pltpu.VMEM(coarse_shape, jnp.float32)),
         in_specs=[hbm, hbm, hbm],
         out_specs=(vmem, vmem),
-        scratch_shapes=[buf(*field.shape)] * 7
+        scratch_shapes=[buf(*field.shape)] * 6
         + [
             whole(*orders.shape), buf(*table.shape),
             buf(2, MODES, 2, MODES, *cells), buf(2, MODES, 2, MODES, *cells),
@@ -822,6 +773,7 @@
             pltpu.SemaphoreType.DMA((2, 3)),
             pltpu.SemaphoreType.DMA((2, RELAYED)),
             pltpu.SemaphoreType.DMA((2, RELAYED)),
+            pltpu.SemaphoreType.REGULAR((2,)),
         ],
         compiler_params=pltpu.CompilerParams(collective_id=0, has_side_effects=True),
         name="smoother",

time: 17.5 us -> 16 us (0.914)
  the two profiles are of different devices: /device:TPU:0 before, /device:TPU:3 now
where the time goes in v4:
time: 16 us; the launch traced here: 15.8 us
  Pallas kernels  15.2 us (95%)
  between operations  0.64 us (4%)
    pallas_call x1, Pallas kernels, per_device(): pl.pallas_call(functools.partial(kernel, sizes, cells_y, cells_z), out_sh...  14.3 us
    pallas_call x1, Pallas kernels, per_device(): pl.pallas_call(drain, out_shape=(jax.ShapeDtypeStruct(field.shape, jnp.fl...  0.91 us

profile of v4, /device:TPU:3, one launch (start us, length us, event | category | flops | bytes accessed | tf_op | source)
XLA Modules:
  0.0 15.8 jit_solution(5539380752129720193)
XLA Ops:
  0.6 14.3 %smoother.1 = (f32[7,7,7,4,128]{4,3,2,1,0:T(4,128)S(1)}, f32[1,4,256]{2,1,0:T(4,128)S(1)}) custom-call(f32[7,7,7,4,128]{4,3,2,1,0:T(4,128)} %bitcast.4, s32[1,4,128]{2,1,0:T(4,128)} %orders_hbm.1, f32[7,7,7,1,128]{4,3,2,1,0:T(1,128)} %constant.2.clone.table_hbm), custom_call_target="tpu_custom_call" | custom-call | tf_op jit(solution)/shard_map/smoother/pallas_call | solution.py:748
  14.9 0.9 %drain.1 = (f32[7,7,7,4,128]{4,3,2,1,0:T(4,128)}, f32[1,4,256]{2,1,0:T(4,128)}) custom-call(f32[7,7,7,4,128]{4,3,2,1,0:T(4,128)S(1)} %get-tuple-element.6.smooth, f32[1,4,256]{2,1,0:T(4,128)S(1)} %get-tuple-element.7.coarse), custom_call_target="tpu_custom_call" | custom-call | tf_op jit(solution)/shard_map/drain/pallas_call | solution.py:781

commit v5 on v4

--- a/solution.py
+++ b/solution.py
@@ -120,7 +120,7 @@
 Y_PARTS = ((slice(0, 2), slice(0, MODES)), (slice(2, MODES), slice(0, 2)), (slice(2, MODES), slice(2, MODES)))
 REACH = range(-2, 4)
 CARRIES = (
-    (3, 1), (2, 1), (-2, 1), (1, 1), (-1, 1), (2, -1), (1, -1), (-1, -1),
+    (1, 1), (-1, 1), (1, -1), (-1, -1), (3, 1), (2, 1), (-2, 1), (2, -1),
     (3, 0), (2, 0), (-2, 0), (1, 0), (-1, 0), (0, 1), (0, -1),
 )
 
@@ -130,7 +130,7 @@
     rhs, first, acc, coef, ghost_up, ghost_down, orders_ref, table_ref,
     xs, xr, ys, yr, zs, zr, y_up, y_down,
     order_line, order_x, order_y, order_z, order_xy, order_xz, order_far, order_tile, pads,
-    out_mid, out_high, out_low, in_mid, in_high, in_low, column,
+    out_mid, out_high, out_low, in_mid, in_high, in_low, far_mid, far_high, far_low, column,
     relay, local_sem, send_sem, recv_sem, x_send, x_recv, y_send, y_recv, relay_in, relay_out, met,
 ):
     nx, ny, nz = sizes
@@ -160,6 +160,12 @@
         return ((x + dx, y + dy, z), ok_to, (x - dx, y - dy, z), ok_from)
 
     carries = [offset(dx, dy) + (dx, dy) for dx, dy in CARRIES]
+    collects = z == nz - 1
+    direct = []
+    for dx, dy in CARRIES + ((0, 0),):
+        to, ok_to, back, ok_from = offset(dx, dy)
+        to = to[:2] + (nz - 1,)
+        direct.append((to, ok_to & jnp.logical_not(collects), back, ok_from, dx, dy))
     columns = []
     for r in range(1, nz):
         source = lax.rem(z - r + nz, nz)
@@ -285,6 +291,19 @@
         src, dst = targets[dy]
         at = dx + 1 if dy < 0 else dx + 2
         return src.at[at], dst.at[at]
+
+    far_of = {0: far_mid, 1: far_high, -1: far_low}
+
+    def direct_refs(dx, dy, source):
+        at = dx + 1 if dy < 0 else dx + 2
+        return targets[dy][0].at[at], far_of[dy].at[at, source]
+
+    for _, _, _, ok_from, dx, dy in direct:
+
+        @pl.when(jnp.logical_not(ok_from))
+        def _(dx=dx, dy=dy):
+            dst = far_of[dy].at[dx + 1 if dy < 0 else dx + 2]
+            dst[...] = jnp.zeros(dst.shape, jnp.float32)
 
     for _, _, _, ok_from, dx, dy in carries:
 
@@ -599,6 +618,12 @@
     tile_orders, edge_orders = surroundings(0)
     spread(acc, 0, rhs, tile_orders, order_x[1], order_x[0], edge_orders)
     diagonal_over(receive)
+
+    @pl.when(collects)
+    def _():
+        for zz in range(nz - 1):
+            pl.semaphore_signal(met.at[2], inc=1, device_id=(x, y, zz), device_id_type=MESH)
+
     forward(2)
     tile_orders, edge_orders = surroundings(1)
     spread(ghost_up, 1, None, tile_orders, orders, order_far[0], edge_orders)
@@ -607,7 +632,12 @@
 
     row_lane = lane[0]
     sums = {}
-    for dx in REACH:
+    def carries_of(dx):
+        for number, entry in enumerate(carries):
+            if entry[4] == dx:
+                start(entry, 24 + number, *carry_refs(*entry[4:]))
+
+    for dx in (1, -1, 2, 3, -2, 0):
         pair = []
         for k in range(2):
             parts = [layers[dx, k]] if (dx, k) in layers else []
@@ -625,14 +655,21 @@
         for part, value in enumerate((inside, beyond)):
             if dx == 0:
                 sums[part] = value[1 : cells_y + 1]
-            else:
-                out_mid[dx + 2, part] = value[1 : cells_y + 1]
+            out_mid[dx + 2, part] = value[1 : cells_y + 1]
             out_high[dx + 2, part] = value[cells_y + 1 : cells_y + 3]
             if -1 <= dx <= 2:
                 out_low[dx + 1, part] = value[0:1]
-
-    for number, entry in enumerate(carries):
-        start(entry, 24 + number, *carry_refs(*entry[4:]))
+        carries_of(dx)
+
+    direct_slot = 24 + len(carries) + len(columns)
+
+    @pl.when(jnp.logical_not(collects))
+    def _():
+        pl.semaphore_wait(met.at[2], 1)
+
+    for number, entry in enumerate(direct):
+        start(entry, direct_slot + number * nz + z, *direct_refs(*entry[4:], z))
+
     forward(3)
     y_over(receive, 2)
     y_flux_part(slice(2, MODES))
@@ -645,8 +682,6 @@
         for a in range(MODES):
             smooth[a, b] = acc[a, b] + coef[a, b] * term(a)
 
-    loop(x_flux, RELAYED)
-
     for stage, axis in ((0, 2), (1, 0), (1, 1), (1, 2)):
         over(finish, stage, axis)
     for part in range(3):
@@ -665,6 +700,9 @@
             @pl.when(relays[side][3])
             def _():
                 from_relay(side, b, relays[side][4]).wait_send()
+
+    loop(x_flux, RELAYED)
+    loop(x_flux, 0, RELAYED)
 
     for number, entry in enumerate(carries):
         receive(entry, 24 + number, *carry_refs(*entry[4:]))
@@ -685,15 +723,39 @@
         at = entry[4] if arriving else z
         return remote(column.at[at], column.at[at], 24 + len(carries) + number, entry[0])
 
-    for number in range(len(columns)):
-        gather(number, False).start()
-    loop(x_flux, 0, RELAYED)
+    def columns_over(action, arriving):
+        for number, entry in enumerate(columns):
+            to_collector = collects if arriving else entry[0][2] == nz - 1
+
+            @pl.when((x > 0) & jnp.logical_not(to_collector))
+            def _(number=number):
+                action(number)
+
+    columns_over(lambda number: gather(number, False).start(), False)
     for number, entry in enumerate(carries):
         finish(entry, 24 + number, *carry_refs(*entry[4:]))
-    for number in range(len(columns)):
-        gather(number, True).wait_recv()
-    for number in range(len(columns)):
-        gather(number, False).wait_send()
+    for number, entry in enumerate(direct):
+        finish(entry, direct_slot + number * nz + z, *direct_refs(*entry[4:], z))
+    @pl.when(collects)
+    def _():
+        for number, (to, _, back, ok_from, dx, dy) in enumerate(direct):
+            for zz in range(nz - 1):
+                slot = direct_slot + number * nz + zz
+                receive((to, None, back, ok_from), slot, *direct_refs(dx, dy, zz))
+        for zz in range(nz - 1):
+            for part in range(2):
+                column[zz, part] = functools.reduce(
+                    lambda p, q: p + q, [far_mid[at, zz, part] for at in range(6)]
+                )
+                column[zz, part, 0:2] += functools.reduce(
+                    lambda p, q: p + q, [far_high[at, zz, part] for at in range(6)]
+                )
+                column[zz, part, cells_y - 1 : cells_y] += functools.reduce(
+                    lambda p, q: p + q, [far_low[at, zz, part] for at in range(4)]
+                )
+
+    columns_over(lambda number: gather(number, True).wait_recv(), True)
+    columns_over(lambda number: gather(number, False).wait_send(), False)
 
     row = lax.broadcasted_iota(jnp.int32, (cells_y, cells_z), 0)
     spot = lax.broadcasted_iota(jnp.int32, (cells_y, cells_z), 1)
@@ -741,7 +803,7 @@
     def whole(*shape):
         return pltpu.VMEM(shape, jnp.int32)
 
-    slots = 24 + len(CARRIES) + nz - 1
+    slots = 24 + len(CARRIES) + nz - 1 + (len(CARRIES) + 1) * nz
     coarse_shape = (1, cells_y, nz * cells_z)
     vmem = pl.BlockSpec(memory_space=pltpu.VMEM)
     hbm = pl.BlockSpec(memory_space=pltpu.HBM)
@@ -762,6 +824,7 @@
             buf(112, tall, cells_z),
             buf(6, 2, *cells), buf(6, 2, 2, cells_z), buf(4, 2, 1, cells_z),
             buf(6, 2, *cells), buf(6, 2, 2, cells_z), buf(4, 2, 1, cells_z),
+            buf(6, nz, 2, *cells), buf(6, nz, 2, 2, cells_z), buf(4, nz, 2, 1, cells_z),
             buf(nz, 2, *cells),
             buf(2, RELAYED, 2, MODES, *cells),
             pltpu.SemaphoreType.DMA((MODES + 2,)),
@@ -773,7 +836,7 @@
             pltpu.SemaphoreType.DMA((2, 3)),
             pltpu.SemaphoreType.DMA((2, RELAYED)),
             pltpu.SemaphoreType.DMA((2, RELAYED)),
-            pltpu.SemaphoreType.REGULAR((2,)),
+            pltpu.SemaphoreType.REGULAR((3,)),
         ],
         compiler_params=pltpu.CompilerParams(collective_id=0, has_side_effects=True),
         name="smoother",

time: 16 us -> 15.8 us (0.988)
  the two profiles are of different devices: /device:TPU:3 before, /device:TPU:0 now
where the time goes in v5:
time: 15.8 us; the launch traced here: 15.6 us
  Pallas kernels  15 us (95%)
  between operations  0.64 us (4%)
    pallas_call x1, Pallas kernels, per_device(): pl.pallas_call(functools.partial(kernel, sizes, cells_y, cells_z), out_sh...  14.1 us
    pallas_call x1, Pallas kernels, per_device(): pl.pallas_call(drain, out_shape=(jax.ShapeDtypeStruct(field.shape, jnp.fl...  0.91 us

profile of v5, /device:TPU:0, one launch (start us, length us, event | category | flops | bytes accessed | tf_op | source)
XLA Modules:
  0.0 15.6 jit_solution(14698370096418045557)
XLA Ops:
  0.6 14.1 %smoother.1 = (f32[7,7,7,4,128]{4,3,2,1,0:T(4,128)S(1)}, f32[1,4,256]{2,1,0:T(4,128)S(1)}) custom-call(f32[7,7,7,4,128]{4,3,2,1,0:T(4,128)} %bitcast.4, s32[1,4,128]{2,1,0:T(4,128)} %orders_hbm.1, f32[7,7,7,1,128]{4,3,2,1,0:T(1,128)} %constant.2.clone.table_hbm), custom_call_target="tpu_custom_call" | custom-call | tf_op jit(solution)/shard_map/smoother/pallas_call | solution.py:810
  14.7 0.9 %drain.1 = (f32[7,7,7,4,128]{4,3,2,1,0:T(4,128)}, f32[1,4,256]{2,1,0:T(4,128)}) custom-call(f32[7,7,7,4,128]{4,3,2,1,0:T(4,128)S(1)} %get-tuple-element.6.smooth, f32[1,4,256]{2,1,0:T(4,128)S(1)} %get-tuple-element.7.coarse), custom_call_target="tpu_custom_call" | custom-call | tf_op jit(solution)/shard_map/drain/pallas_call | solution.py:844

commit v6 on v5

--- a/solution.py
+++ b/solution.py
@@ -417,13 +417,16 @@
                 else:
                     pl.semaphore_wait(met.at[side], 1)
 
-    loop(x_traces, 0, 2)
+    loop(x_traces, 0, 5)
     pl.semaphore_wait(barrier, expected)
     meet("tell")
     over(start, 1, 0)
+    over(start, 1, 1)
+    over(start, 1, 2)
     x_start(0)
     x_start(1)
-    loop(x_traces, 2)
+    x_start(2)
+    loop(x_traces, 5)
 
     def y_faces(a, values, send, up_buf, down_buf):
         down, up = traces(values)
@@ -465,15 +468,12 @@
     y_over(start, 0)
     loop(y_traces, 2)
     y_over(start, 1)
-    over(start, 1, 1)
     meet("hear")
     diagonal_over(start)
-    x_start(2)
-    over(start, 1, 2)
+    x_start(3)
     y_over(start, 2)
     loop(lambda a: z_faces(a, [first[a, :, e] for e in range(MODES)], zs))
     over(start, 0, 2)
-    x_start(3)
 
     def predict(a, b, part, total):
         right = rhs[a, b, part]

time: 15.8 us -> 15.6 us (0.987)
  Pallas kernels: 15 us -> 14.7 us
    pallas_call x1, Pallas kernels: 14.1 us -> 13.8 us  [per_device(): pl.pallas_call(functools.partial(kernel, sizes, cells_y, cells_z), out_sh...]
where the time goes in v6:
time: 15.6 us; the launch traced here: 15.3 us
  Pallas kernels  14.7 us (94%)
  between operations  0.64 us (4%)
    pallas_call x1, Pallas kernels, per_device(): pl.pallas_call(functools.partial(kernel, sizes, cells_y, cells_z), out_sh...  13.8 us
    pallas_call x1, Pallas kernels, per_device(): pl.pallas_call(drain, out_shape=(jax.ShapeDtypeStruct(field.shape, jnp.fl...  0.91 us

profile of v6, /device:TPU:0, one launch (start us, length us, event | category | flops | bytes accessed | tf_op | source)
XLA Modules:
  0.0 15.3 jit_solution(16823925168493071780)
XLA Ops:
  0.6 13.8 %smoother.1 = (f32[7,7,7,4,128]{4,3,2,1,0:T(4,128)S(1)}, f32[1,4,256]{2,1,0:T(4,128)S(1)}) custom-call(f32[7,7,7,4,128]{4,3,2,1,0:T(4,128)} %bitcast.4, s32[1,4,128]{2,1,0:T(4,128)} %orders_hbm.1, f32[7,7,7,1,128]{4,3,2,1,0:T(1,128)} %constant.2.clone.table_hbm), custom_call_target="tpu_custom_call" | custom-call | tf_op jit(solution)/shard_map/smoother/pallas_call | solution.py:810
  14.4 0.9 %drain.1 = (f32[7,7,7,4,128]{4,3,2,1,0:T(4,128)}, f32[1,4,256]{2,1,0:T(4,128)}) custom-call(f32[7,7,7,4,128]{4,3,2,1,0:T(4,128)S(1)} %get-tuple-element.6.smooth, f32[1,4,256]{2,1,0:T(4,128)S(1)} %get-tuple-element.7.coarse), custom_call_target="tpu_custom_call" | custom-call | tf_op jit(solution)/shard_map/drain/pallas_call | solution.py:844

commit v7 on v6

--- a/solution.py
+++ b/solution.py
@@ -536,7 +536,7 @@
     def gather_into(where_to, key, value):
         where_to[key] = where_to[key] + value if key in where_to else value
 
-    def spread(values, shift, forced, tile_orders, low_orders, high_orders, edge_orders):
+    def spread(values, shift, forced):
         centre, edge, x_low, x_high, y_low, y_high = {}, {}, {}, {}, {}, {}
         for b in range(2):
             line = [values[a, b, 0:2] for a in range(MODES)]
@@ -546,8 +546,8 @@
                 below, above = one_sided(down, a, False), one_sided(up, a, True)
                 for e in range(2):
                     centre[a, b, e] = forced[a, b, e] - own[e] if forced is not None else -own[e]
-                    x_low[a, b, e] = jnp.where(low_orders >= max(a, b, e), -below[e], 0.0)
-                    x_high[a, b, e] = jnp.where(high_orders >= max(a, b, e), -above[e], 0.0)
+                    x_low[a, b, e] = -below[e]
+                    x_high[a, b, e] = -above[e]
         for a in range(2):
             line = [values[a, b, 0:2] for b in range(MODES)]
             down, up = traces(line)
@@ -567,18 +567,28 @@
                 own = own_row(e, line) + inner
                 for b in range(2):
                     centre[a, b, e] = centre[a, b, e] - own[b]
-                    edge[a, b, e] = jnp.where(edge_orders >= max(a, b, e), -outer[b], 0.0)
-        resid = {}
-        for key in OCTET:
-            total = padded(centre[key], 1) - padded(y_low[key], 0) - padded(y_high[key], 2)
-            resid[key] = jnp.where(tile_orders >= max(key), total, 0.0)
-        resid, edge, x_low, x_high = corners(resid), corners(edge), corners(x_low), corners(x_high)
-        for i, j, k in OCTET:
-            moved = pltpu.roll(resid[i, j, k], 1, 0) if j else resid[i, j, k]
-            gather_into(layers, (shift + i, k), moved)
-            gather_into(border, (shift + i, j, k), edge[i, j, k])
-            gather_into(near, (shift - 1 + i, j, k), x_low[i, j, k])
-            gather_into(near, (shift + 1 + i, j, k), x_high[i, j, k])
+                    edge[a, b, e] = -outer[b]
+        resid = {
+            key: padded(centre[key], 1) - padded(y_low[key], 0) - padded(y_high[key], 2)
+            for key in OCTET
+        }
+
+        def masked(parts, degrees):
+            return corners(
+                {key: jnp.where(degrees >= max(key), parts[key], 0.0) for key in OCTET}
+            )
+
+        def settle_sums(tile_orders, low_orders, high_orders, edge_orders):
+            cells, rim = masked(resid, tile_orders), masked(edge, edge_orders)
+            low, high = masked(x_low, low_orders), masked(x_high, high_orders)
+            for i, j, k in OCTET:
+                moved = pltpu.roll(cells[i, j, k], 1, 0) if j else cells[i, j, k]
+                gather_into(layers, (shift + i, k), moved)
+                gather_into(border, (shift + i, j, k), rim[i, j, k])
+                gather_into(near, (shift - 1 + i, j, k), low[i, j, k])
+                gather_into(near, (shift + 1 + i, j, k), high[i, j, k])
+
+        return settle_sums
 
     def ghost(values, side, other_orders):
         def put(a, b, high):
@@ -616,7 +626,9 @@
     y_flux_part(slice(0, 2))
     forward(1)
     tile_orders, edge_orders = surroundings(0)
-    spread(acc, 0, rhs, tile_orders, order_x[1], order_x[0], edge_orders)
+    spread(acc, 0, rhs)(tile_orders, order_x[1], order_x[0], edge_orders)
+    raised = spread(ghost_up, 1, None)
+    lowered = spread(ghost_down, -1, None)
     diagonal_over(receive)
 
     @pl.when(collects)
@@ -626,9 +638,9 @@
 
     forward(2)
     tile_orders, edge_orders = surroundings(1)
-    spread(ghost_up, 1, None, tile_orders, orders, order_far[0], edge_orders)
+    raised(tile_orders, orders, order_far[0], edge_orders)
     tile_orders, edge_orders = surroundings(2)
-    spread(ghost_down, -1, None, tile_orders, order_far[1], orders, edge_orders)
+    lowered(tile_orders, order_far[1], orders, edge_orders)
 
     row_lane = lane[0]
     sums = {}

time: 15.6 us -> 15.5 us (level)
  no operation moved by 1% of the time
where the time goes in v7:
time: 15.5 us; the launch traced here: 15.3 us
  Pallas kernels  14.7 us (95%)
  between operations  0.64 us (4%)
    pallas_call x1, Pallas kernels, per_device(): pl.pallas_call(functools.partial(kernel, sizes, cells_y, cells_z), out_sh...  13.8 us
    pallas_call x1, Pallas kernels, per_device(): pl.pallas_call(drain, out_shape=(jax.ShapeDtypeStruct(field.shape, jnp.fl...  0.91 us

profile of v7, /device:TPU:0, one launch (start us, length us, event | category | flops | bytes accessed | tf_op | source)
XLA Modules:
  0.0 15.3 jit_solution(3499130464958336280)
XLA Ops:
  0.6 13.8 %smoother.1 = (f32[7,7,7,4,128]{4,3,2,1,0:T(4,128)S(1)}, f32[1,4,256]{2,1,0:T(4,128)S(1)}) custom-call(f32[7,7,7,4,128]{4,3,2,1,0:T(4,128)} %bitcast.4, s32[1,4,128]{2,1,0:T(4,128)} %orders_hbm.1, f32[7,7,7,1,128]{4,3,2,1,0:T(1,128)} %constant.2.clone.table_hbm), custom_call_target="tpu_custom_call" | custom-call | tf_op jit(solution)/shard_map/smoother/pallas_call | solution.py:822
  14.4 0.9 %drain.1 = (f32[7,7,7,4,128]{4,3,2,1,0:T(4,128)}, f32[1,4,256]{2,1,0:T(4,128)}) custom-call(f32[7,7,7,4,128]{4,3,2,1,0:T(4,128)S(1)} %get-tuple-element.6.smooth, f32[1,4,256]{2,1,0:T(4,128)S(1)} %get-tuple-element.7.coarse), custom_call_target="tpu_custom_call" | custom-call | tf_op jit(solution)/shard_map/drain/pallas_call | solution.py:856

commit v8 on v7

--- a/solution.py
+++ b/solution.py
@@ -644,6 +644,17 @@
 
     row_lane = lane[0]
     sums = {}
+    direct_slot = 24 + len(carries) + len(columns)
+
+    @pl.when(jnp.logical_not(collects))
+    def _():
+        pl.semaphore_wait(met.at[2], 1)
+
+    def direct_of(dx):
+        for number, entry in enumerate(direct):
+            if entry[4] == dx:
+                start(entry, direct_slot + number * nz + z, *direct_refs(*entry[4:], z))
+
     def carries_of(dx):
         for number, entry in enumerate(carries):
             if entry[4] == dx:
@@ -671,16 +682,8 @@
             out_high[dx + 2, part] = value[cells_y + 1 : cells_y + 3]
             if -1 <= dx <= 2:
                 out_low[dx + 1, part] = value[0:1]
+        direct_of(dx)
         carries_of(dx)
-
-    direct_slot = 24 + len(carries) + len(columns)
-
-    @pl.when(jnp.logical_not(collects))
-    def _():
-        pl.semaphore_wait(met.at[2], 1)
-
-    for number, entry in enumerate(direct):
-        start(entry, direct_slot + number * nz + z, *direct_refs(*entry[4:], z))
 
     forward(3)
     y_over(receive, 2)

time: 15.5 us -> 15.5 us (level)
  no operation moved by 1% of the time
where the time goes in v8:
time: 15.5 us; the launch traced here: 15.3 us
  Pallas kernels  14.7 us (95%)
  between operations  0.64 us (4%)
    pallas_call x1, Pallas kernels, per_device(): pl.pallas_call(functools.partial(kernel, sizes, cells_y, cells_z), out_sh...  13.8 us
    pallas_call x1, Pallas kernels, per_device(): pl.pallas_call(drain, out_shape=(jax.ShapeDtypeStruct(field.shape, jnp.fl...  0.91 us

profile of v8, /device:TPU:0, one launch (start us, length us, event | category | flops | bytes accessed | tf_op | source)
XLA Modules:
  0.0 15.3 jit_solution(2466367673403854211)
XLA Ops:
  0.6 13.8 %smoother.1 = (f32[7,7,7,4,128]{4,3,2,1,0:T(4,128)S(1)}, f32[1,4,256]{2,1,0:T(4,128)S(1)}) custom-call(f32[7,7,7,4,128]{4,3,2,1,0:T(4,128)} %bitcast.4, s32[1,4,128]{2,1,0:T(4,128)} %orders_hbm.1, f32[7,7,7,1,128]{4,3,2,1,0:T(1,128)} %constant.2.clone.table_hbm), custom_call_target="tpu_custom_call" | custom-call | tf_op jit(solution)/shard_map/smoother/pallas_call | solution.py:825
  14.4 0.9 %drain.1 = (f32[7,7,7,4,128]{4,3,2,1,0:T(4,128)}, f32[1,4,256]{2,1,0:T(4,128)}) custom-call(f32[7,7,7,4,128]{4,3,2,1,0:T(4,128)S(1)} %get-tuple-element.6.smooth, f32[1,4,256]{2,1,0:T(4,128)S(1)} %get-tuple-element.7.coarse), custom_call_target="tpu_custom_call" | custom-call | tf_op jit(solution)/shard_map/drain/pallas_call | solution.py:859

commit v9 on v8

--- a/solution.py
+++ b/solution.py
@@ -717,6 +717,11 @@
                 from_relay(side, b, relays[side][4]).wait_send()
 
     loop(x_flux, RELAYED)
+    for number, entry in enumerate(carries):
+        finish(entry, 24 + number, *carry_refs(*entry[4:]))
+    for number, entry in enumerate(direct):
+        finish(entry, direct_slot + number * nz + z, *direct_refs(*entry[4:], z))
+
     loop(x_flux, 0, RELAYED)
 
     for number, entry in enumerate(carries):
@@ -747,10 +752,6 @@
                 action(number)
 
     columns_over(lambda number: gather(number, False).start(), False)
-    for number, entry in enumerate(carries):
-        finish(entry, 24 + number, *carry_refs(*entry[4:]))
-    for number, entry in enumerate(direct):
-        finish(entry, direct_slot + number * nz + z, *direct_refs(*entry[4:], z))
     @pl.when(collects)
     def _():
         for number, (to, _, back, ok_from, dx, dy) in enumerate(direct):

time: 15.5 us -> 15.5 us (level)
  no operation moved by 1% of the time
where the time goes in v9:
time: 15.5 us; the launch traced here: 15.3 us
  Pallas kernels  14.7 us (95%)
  between operations  0.64 us (4%)
    pallas_call x1, Pallas kernels, per_device(): pl.pallas_call(functools.partial(kernel, sizes, cells_y, cells_z), out_sh...  13.8 us
    pallas_call x1, Pallas kernels, per_device(): pl.pallas_call(drain, out_shape=(jax.ShapeDtypeStruct(field.shape, jnp.fl...  0.91 us

profile of v9, /device:TPU:0, one launch (start us, length us, event | category | flops | bytes accessed | tf_op | source)
XLA Modules:
  0.0 15.3 jit_solution(11130339581763857088)
XLA Ops:
  0.6 13.8 %smoother.1 = (f32[7,7,7,4,128]{4,3,2,1,0:T(4,128)S(1)}, f32[1,4,256]{2,1,0:T(4,128)S(1)}) custom-call(f32[7,7,7,4,128]{4,3,2,1,0:T(4,128)} %bitcast.4, s32[1,4,128]{2,1,0:T(4,128)} %orders_hbm.1, f32[7,7,7,1,128]{4,3,2,1,0:T(1,128)} %constant.2.clone.table_hbm), custom_call_target="tpu_custom_call" | custom-call | tf_op jit(solution)/shard_map/smoother/pallas_call | solution.py:826
  14.4 0.9 %drain.1 = (f32[7,7,7,4,128]{4,3,2,1,0:T(4,128)}, f32[1,4,256]{2,1,0:T(4,128)}) custom-call(f32[7,7,7,4,128]{4,3,2,1,0:T(4,128)S(1)} %get-tuple-element.6.smooth, f32[1,4,256]{2,1,0:T(4,128)S(1)} %get-tuple-element.7.coarse), custom_call_target="tpu_custom_call" | custom-call | tf_op jit(solution)/shard_map/drain/pallas_call | solution.py:860
